TPU v7x, 32 devices: a whole 2x2x4 slice. The times are simulated.
32 devices in a mesh: wide: 8 (over z, y), narrow: 4 (over x, core).
Axes of the slice: x: 2, y: 2, z: 4, core: 2. Of those that a mesh axis runs over, the one named last changes fastest.
Arguments:
- mobility: float32 [128, 64, 256], P('wide', 'narrow'), may hold values from 0.2 to 5
- sav_vector: float32 [128, 64, 256], P('wide', 'narrow'), may hold values from -8 to 8
- cotangent: float32 [128, 64, 256], P('wide', 'narrow'), may hold values from -8 to 8
Outputs:
- adjoint: float32 [128, 64, 256], P('wide', 'narrow')
All inputs are finite; a program needn't handle non-finite values.
Results may differ from a plain program's by a relative error of at most 0.0019.
Values sent between devices are 32-bit elements; how exact they have to be, the bound alone decides.
A program may use at most 128 MiB of HBM per device.

v0:
```python
import jax
import jax.numpy as jnp
from jax import lax
from jax.sharding import PartitionSpec as P

LEVELS = 5


DAMPING = 0.8
BASE_TAU = 16.0


def with_halo(block, sides, width):
    for axis, dim in sides:
        count = lax.axis_size(axis)
        forward = [(i, i + 1) for i in range(count - 1)]
        backward = [(target, source) for source, target in forward]
        low = lax.ppermute(
            lax.slice_in_dim(block, block.shape[dim] - width, None, axis=dim), axis, forward
        )
        high = lax.ppermute(lax.slice_in_dim(block, 0, width, axis=dim), axis, backward)
        block = jnp.concatenate([low, block, high], axis=dim)
    return block


def face_terms(padded, tau):
    center = padded[1:-1, 1:-1, 1:-1]
    others = [
        padded[2:, 1:-1, 1:-1],
        padded[:-2, 1:-1, 1:-1],
        padded[1:-1, 2:, 1:-1],
        padded[1:-1, :-2, 1:-1],
        padded[1:-1, 1:-1, 2:],
        padded[1:-1, 1:-1, :-2],
    ]
    couplings = jnp.stack([0.5 * tau * (center + other) for other in others]).astype(jnp.bfloat16)
    diagonal = jnp.float32(1.0) + couplings[0].astype(jnp.float32)
    for index in range(1, 6):
        diagonal = diagonal + couplings[index].astype(jnp.float32)
    return (couplings, diagonal)


def coarsen(values):
    count, size_x, size_y, size_z = values.shape
    blocks = values.reshape(count, size_x // 2, 2, size_y // 2, 2, size_z // 2, 2)
    return blocks.mean(axis=(2, 4, 6))


def refine(values):
    return jnp.repeat(jnp.repeat(jnp.repeat(values, 2, axis=1), 2, axis=2), 2, axis=3)


def stencil(padded, couplings, diagonal):
    center = padded[:, 1:-1, 1:-1, 1:-1]
    others = [
        padded[:, 2:, 1:-1, 1:-1],
        padded[:, :-2, 1:-1, 1:-1],
        padded[:, 1:-1, 2:, 1:-1],
        padded[:, 1:-1, :-2, 1:-1],
        padded[:, 1:-1, 1:-1, 2:],
        padded[:, 1:-1, 1:-1, :-2],
    ]
    total = couplings[0].astype(jnp.float32)[None] * others[0]
    for index in range(1, 6):
        total = total + couplings[index].astype(jnp.float32)[None] * others[index]
    return diagonal[None] * center - total


def operate(iterate, couplings, diagonal):
    padded = with_halo(iterate, (("wide", 1), ("narrow", 2)), 1)
    padded = jnp.pad(padded, ((0, 0), (0, 0), (0, 0), (1, 1)))
    return stencil(padded, couplings, diagonal)


def relax_once(iterate, source, couplings, diagonal):
    return iterate + DAMPING * (source - operate(iterate, couplings, diagonal)) / diagonal[None]


def multigrid(source, level_index, operators):
    couplings, diagonal = operators[level_index]
    iterate = DAMPING * source / diagonal[None]
    if level_index == LEVELS - 1:
        return relax_once(iterate, source, couplings, diagonal)
    iterate = relax_once(iterate, source, couplings, diagonal)
    residual = source - operate(iterate, couplings, diagonal)
    correction = multigrid(coarsen(residual), level_index + 1, operators)
    iterate = iterate + refine(correction)
    iterate = relax_once(iterate, source, couplings, diagonal)
    return relax_once(iterate, source, couplings, diagonal)


def inner_sums(adjoint_b, sav_vector, cotangent):
    numerator, denominator = lax.psum(
        (jnp.sum(adjoint_b * cotangent), jnp.sum(sav_vector * adjoint_b)), ("wide", "narrow")
    )
    return numerator / (1.0 + denominator)


def per_device(mobility, sav_vector, cotangent):
    operators = []
    mobile = mobility
    for level_index in range(LEVELS):
        tau = BASE_TAU / 4.0**level_index
        padded = with_halo(mobile, (("wide", 0), ("narrow", 1)), 1)
        padded = jnp.pad(padded, ((0, 0), (0, 0), (1, 1)))
        operators.append(face_terms(padded, tau))
        if level_index + 1 < LEVELS:
            mobile = coarsen(mobile[None])[0]
    paired = multigrid(jnp.stack([sav_vector, cotangent]), 0, operators)
    sav_ratio = inner_sums(paired[0], sav_vector, cotangent)
    return paired[1] - sav_ratio * paired[0]


def solution(mesh):
    in_specs = (P("wide", "narrow", None), P("wide", "narrow", None), P("wide", "narrow", None))
    out_specs = P("wide", "narrow", None)
    return jax.shard_map(
        per_device, mesh=mesh, in_specs=in_specs, out_specs=out_specs, check_vma=False
    )
```

profile of v0, /device:TPU:1, one launch (start us, length us, event | category | flops | bytes accessed | tf_op | source)
XLA Modules:
  0.0 459.0 jit_solution(12228159161160099381)
XLA Ops:
  2.0 4.6 %collective-permute-start.1 = (f32[1,16,256]{2,1,0:T(8,128)S(1)}, f32[1,16,256]{2,1,0:T(8,128)S(1)}, u32[]{:S(2)}, u32[]{:S(2)}) collective-permute-start(f32[1,16,256]{2,1,0:T(8,128)S(1)} %get-tuple-element.55), channel_id=1, source_target_pairs={{0,4},{4,8},{8,12},{12,16},{16,20},{20,24},{24,28},{1,5},{5,9},{9,... | collective-permute-start | bytes 49160 | tf_op jit(solution)/shard_map/ppermute | solution.py:18
  6.6 18.9 %reshape_broadcast_in_dim.3 = f32[8,2,8,2,128,2]{5,4,3,2,1,0:T(8,128)} reshape(f32[16,16,256]{2,1,0:T(8,128)} %param.3) | data formatting | bytes 524288 | tf_op jit(solution)/shard_map/reshape;broadcast_in_dim | solution.py:45
  25.5 7.0 %reduce_sum.105 = f32[8,8,128]{2,1,0:T(8,128)S(1)} reduce(f32[8,2,8,2,128,2]{5,4,3,2,1,0:T(8,128)} %reshape_broadcast_in_dim.3, f32[]{:T(128)} %constant.16.clone.1), dimensions={1,3,5}, to_apply=%region_1.2 | reduce | flops 57344 | bytes 294916 | tf_op jit(solution)/shard_map/reduce_sum | solution.py:46
  33.8 4.9 %collective-permute-start.13 = (f32[1,8,128]{2,1,0:T(8,128)S(1)}, f32[1,8,128]{2,1,0:T(8,128)S(1)}, u32[]{:S(2)}, u32[]{:S(2)}) collective-permute-start(f32[1,8,128]{2,1,0:T(8,128)S(1)} %get-tuple-element.75), channel_id=1, source_target_pairs={{0,4},{4,8},{8,12},{12,16},{16,20},{20,24},{24,28},{1,5},{5,9},{9,... | collective-permute-start | bytes 12296 | tf_op jit(solution)/shard_map/ppermute | solution.py:18
  52.8 5.8 %collective-permute-start.5 = (f32[2,1,16,256]{3,2,1,0:T(8,128)S(1)}, f32[2,1,16,256]{3,2,1,0:T(8,128)S(1)}, u32[]{:S(2)}, u32[]{:S(2)}) collective-permute-start(f32[2,1,16,256]{3,2,1,0:T(8,128)S(1)} %get-tuple-element.51), channel_id=1, source_target_pairs={{0,4},{4,8},{8,12},{12,16},{16,20},{20,24},{24,28},{1,5},{5,9},{9,... | collective-permute-start | bytes 98312 | tf_op jit(solution)/shard_map/ppermute | solution.py:18
  58.6 4.3 collective-permute-start.25
  70.6 3.6 collective-permute-start.15
  76.9 4.0 collective-permute-start.9
  84.0 3.6 collective-permute-start.11
  90.0 34.8 %reshape.384 = f32[2,8,2,8,2,128,2]{6,5,4,3,2,1,0:T(8,128)} reshape(f32[2,16,16,256]{3,2,1,0:T(8,128)S(1)} %fusion.32) | data formatting | bytes 1048576 | tf_op jit(solution)/shard_map/reshape | solution.py:45
  124.9 12.2 %reduce_sum.104 = f32[2,8,8,128]{3,2,1,0:T(8,128)S(1)} reduce(f32[2,8,2,8,2,128,2]{6,5,4,3,2,1,0:T(8,128)} %reshape.384, f32[]{:T(128)} %constant.16.clone.1), dimensions={2,4,6}, to_apply=%region_0.1 | reduce | flops 114688 | bytes 589828 | tf_op jit(solution)/shard_map/reduce_sum | solution.py:46
  138.4 4.9 %collective-permute-start.17 = (f32[2,1,8,128]{3,2,1,0:T(8,128)S(1)}, f32[2,1,8,128]{3,2,1,0:T(8,128)S(1)}, u32[]{:S(2)}, u32[]{:S(2)}) collective-permute-start(f32[2,1,8,128]{3,2,1,0:T(8,128)S(1)} %get-tuple-element.71), channel_id=1, source_target_pairs={{0,4},{4,8},{8,12},{12,16},{16,20},{20,24},{24,28},{1,5},{5,9},{9,... | collective-permute-start | bytes 24584 | tf_op jit(solution)/shard_map/ppermute | solution.py:18
  144.6 5.2 %collective-permute-start.37 = (f32[1,2,32]{2,1,0:T(2,128)S(1)}, f32[1,2,32]{2,1,0:T(2,128)S(1)}, u32[]{:S(2)}, u32[]{:S(2)}) collective-permute-start(f32[1,2,32]{2,1,0:T(2,128)S(1)} %get-tuple-element.125), channel_id=1, source_target_pairs={{0,4},{4,8},{8,12},{12,16},{16,20},{20,24},{24,28},{1,5},{5,9},{9,... | collective-permute-start | bytes 776 | tf_op jit(solution)/shard_map/ppermute | solution.py:18
  151.8 4.8 %collective-permute-start.19 = (f32[2,10,1,128]{3,0,2,1:T(2,128)S(1)}, f32[2,10,1,128]{3,0,2,1:T(2,128)S(1)}, u32[]{:S(2)}, u32[]{:S(2)}) collective-permute-start(f32[2,10,1,128]{3,0,2,1:T(2,128)S(1)} %copy.408), channel_id=1, source_target_pairs={{0,1},{1,2},{2,3},{4,5},{5,6},{6,7},{8,9},{9,10},{10,11},{12,13},{... | collective-permute-start | bytes 30728 | tf_op jit(solution)/shard_map/ppermute | solution.py:18
  158.6 3.6 collective-permute-start.27
  164.1 5.2 %collective-permute-start.21 = (f32[2,1,8,128]{3,2,1,0:T(8,128)S(1)}, f32[2,1,8,128]{3,2,1,0:T(8,128)S(1)}, u32[]{:S(2)}, u32[]{:S(2)}) collective-permute-start(f32[2,1,8,128]{3,2,1,0:T(8,128)S(1)} %get-tuple-element.69), channel_id=1, source_target_pairs={{0,4},{4,8},{8,12},{12,16},{16,20},{20,24},{24,28},{1,5},{5,9},{9,... | collective-permute-start | bytes 24584 | tf_op jit(solution)/shard_map/ppermute | solution.py:18
  172.1 3.6 collective-permute-start.23
  176.9 5.6 %reshape.385 = f32[2,4,2,4,2,64,2]{6,5,4,3,2,1,0:T(8,128)} reshape(f32[2,8,8,128]{3,2,1,0:T(8,128)S(1)} %fusion.110) | data formatting | bytes 131072 | tf_op jit(solution)/shard_map/reshape | solution.py:45
  186.3 4.9 %collective-permute-start.29 = (f32[2,1,4,64]{3,2,1,0:T(4,128)S(1)}, f32[2,1,4,64]{3,2,1,0:T(4,128)S(1)}, u32[]{:S(2)}, u32[]{:S(2)}) collective-permute-start(f32[2,1,4,64]{3,2,1,0:T(4,128)S(1)} %get-tuple-element.93), channel_id=1, source_target_pairs={{0,4},{4,8},{8,12},{12,16},{16,20},{20,24},{24,28},{1,5},{5,9},{9,... | collective-permute-start | bytes 6152 | tf_op jit(solution)/shard_map/ppermute | solution.py:18
  193.9 5.0 %collective-permute-start.31 = (f32[2,6,1,64]{3,2,1,0:T(1,128)S(1)}, f32[2,6,1,64]{3,2,1,0:T(1,128)S(1)}, u32[]{:S(2)}, u32[]{:S(2)}) collective-permute-start(f32[2,6,1,64]{3,2,1,0:T(1,128)S(1)} %get-tuple-element.85), channel_id=1, source_target_pairs={{0,1},{1,2},{2,3},{4,5},{5,6},{6,7},{8,9},{9,10},{10,11},{12,13},{... | collective-permute-start | bytes 9224 | tf_op jit(solution)/shard_map/ppermute | solution.py:18
  200.9 3.6 collective-permute-start.39
  206.1 5.2 %collective-permute-start.33 = (f32[2,1,4,64]{3,2,1,0:T(4,128)S(1)}, f32[2,1,4,64]{3,2,1,0:T(4,128)S(1)}, u32[]{:S(2)}, u32[]{:S(2)}) collective-permute-start(f32[2,1,4,64]{3,2,1,0:T(4,128)S(1)} %get-tuple-element.91), channel_id=1, source_target_pairs={{0,4},{4,8},{8,12},{12,16},{16,20},{20,24},{24,28},{1,5},{5,9},{9,... | collective-permute-start | bytes 6152 | tf_op jit(solution)/shard_map/ppermute | solution.py:18
  213.9 3.6 collective-permute-start.35
  220.5 5.4 %collective-permute-start.41 = (f32[2,1,2,32]{3,2,1,0:T(2,128)S(1)}, f32[2,1,2,32]{3,2,1,0:T(2,128)S(1)}, u32[]{:S(2)}, u32[]{:S(2)}) collective-permute-start(f32[2,1,2,32]{3,2,1,0:T(2,128)S(1)} %get-tuple-element.118), channel_id=1, source_target_pairs={{0,4},{4,8},{8,12},{12,16},{16,20},{20,24},{24,28},{1,5},{5,9},{9,... | collective-permute-start | bytes 1544 | tf_op jit(solution)/shard_map/ppermute | solution.py:18
  227.3 5.1 %collective-permute-start.49 = (f32[1,1,16]{2,1,0:T(1,128)S(1)}, f32[1,1,16]{2,1,0:T(1,128)S(1)}, u32[]{:S(2)}, u32[]{:S(2)}) collective-permute-start(f32[1,1,16]{2,1,0:T(1,128)S(1)} %multiply_bitcast_fusion), channel_id=1, source_target_pairs={{0,4},{4,8},{8,12},{12,16},{16,20},{20,24},{24,28},{1,5},{5,9},{9,... | collective-permute-start | bytes 200 | tf_op jit(solution)/shard_map/ppermute | solution.py:18
  234.4 4.8 %collective-permute-start.43 = (f32[2,4,1,32]{3,2,1,0:T(1,128)S(1)}, f32[2,4,1,32]{3,2,1,0:T(1,128)S(1)}, u32[]{:S(2)}, u32[]{:S(2)}) collective-permute-start(f32[2,4,1,32]{3,2,1,0:T(1,128)S(1)} %get-tuple-element.103), channel_id=1, source_target_pairs={{0,1},{1,2},{2,3},{4,5},{5,6},{6,7},{8,9},{9,10},{10,11},{12,13},{... | collective-permute-start | bytes 3080 | tf_op jit(solution)/shard_map/ppermute | solution.py:18
  241.2 3.6 collective-permute-start.51
  246.3 5.2 %collective-permute-start.45 = (f32[2,1,2,32]{3,2,1,0:T(2,128)S(1)}, f32[2,1,2,32]{3,2,1,0:T(2,128)S(1)}, u32[]{:S(2)}, u32[]{:S(2)}) collective-permute-start(f32[2,1,2,32]{3,2,1,0:T(2,128)S(1)} %get-tuple-element.116), channel_id=1, source_target_pairs={{0,4},{4,8},{8,12},{12,16},{16,20},{20,24},{24,28},{1,5},{5,9},{9,... | collective-permute-start | bytes 1544 | tf_op jit(solution)/shard_map/ppermute | solution.py:18
  254.1 3.6 collective-permute-start.47
  260.2 4.9 %collective-permute-start.53 = (f32[2,1,1,16]{3,0,2,1:T(2,128)S(1)}, f32[2,1,1,16]{3,0,2,1:T(2,128)S(1)}, u32[]{:S(2)}, u32[]{:S(2)}) collective-permute-start(f32[2,1,1,16]{3,0,2,1:T(2,128)S(1)} %bitcast_divide_fusion), channel_id=1, source_target_pairs={{0,4},{4,8},{8,12},{12,16},{16,20},{20,24},{24,28},{1,5},{5,9},{9,... | collective-permute-start | bytes 392 | tf_op jit(solution)/shard_map/ppermute | solution.py:18
  267.7 5.0 %collective-permute-start.55 = (f32[2,3,1,16]{3,0,2,1:T(2,128)S(1)}, f32[2,3,1,16]{3,0,2,1:T(2,128)S(1)}, u32[]{:S(2)}, u32[]{:S(2)}) collective-permute-start(f32[2,3,1,16]{3,0,2,1:T(2,128)S(1)} %pad_maximum_fusion.196), channel_id=1, source_target_pairs={{0,1},{1,2},{2,3},{4,5},{5,6},{6,7},{8,9},{9,10},{10,11},{12,13},{... | collective-permute-start | bytes 1160 | tf_op jit(solution)/shard_map/ppermute | solution.py:18
  275.2 5.2 %collective-permute-start.57 = (f32[2,1,2,32]{3,2,1,0:T(2,128)S(1)}, f32[2,1,2,32]{3,2,1,0:T(2,128)S(1)}, u32[]{:S(2)}, u32[]{:S(2)}) collective-permute-start(f32[2,1,2,32]{3,2,1,0:T(2,128)S(1)} %get-tuple-element.114), channel_id=1, source_target_pairs={{0,4},{4,8},{8,12},{12,16},{16,20},{20,24},{24,28},{1,5},{5,9},{9,... | collective-permute-start | bytes 1544 | tf_op jit(solution)/shard_map/ppermute | solution.py:18
  283.0 5.0 %collective-permute-start.59 = (f32[2,4,1,32]{3,2,1,0:T(1,128)S(1)}, f32[2,4,1,32]{3,2,1,0:T(1,128)S(1)}, u32[]{:S(2)}, u32[]{:S(2)}) collective-permute-start(f32[2,4,1,32]{3,2,1,0:T(1,128)S(1)} %get-tuple-element.99), channel_id=1, source_target_pairs={{0,1},{1,2},{2,3},{4,5},{5,6},{6,7},{8,9},{9,10},{10,11},{12,13},{... | collective-permute-start | bytes 3080 | tf_op jit(solution)/shard_map/ppermute | solution.py:18
  290.3 5.4 %collective-permute-start.61 = (f32[2,1,2,32]{3,2,1,0:T(2,128)S(1)}, f32[2,1,2,32]{3,2,1,0:T(2,128)S(1)}, u32[]{:S(2)}, u32[]{:S(2)}) collective-permute-start(f32[2,1,2,32]{3,2,1,0:T(2,128)S(1)} %get-tuple-element.112), channel_id=1, source_target_pairs={{0,4},{4,8},{8,12},{12,16},{16,20},{20,24},{24,28},{1,5},{5,9},{9,... | collective-permute-start | bytes 1544 | tf_op jit(solution)/shard_map/ppermute | solution.py:18
  298.4 5.0 %collective-permute-start.63 = (f32[2,4,1,32]{3,2,1,0:T(1,128)S(1)}, f32[2,4,1,32]{3,2,1,0:T(1,128)S(1)}, u32[]{:S(2)}, u32[]{:S(2)}) collective-permute-start(f32[2,4,1,32]{3,2,1,0:T(1,128)S(1)} %get-tuple-element.97), channel_id=1, source_target_pairs={{0,1},{1,2},{2,3},{4,5},{5,6},{6,7},{8,9},{9,10},{10,11},{12,13},{... | collective-permute-start | bytes 3080 | tf_op jit(solution)/shard_map/ppermute | solution.py:18
  306.0 5.4 %collective-permute-start.65 = (f32[2,1,4,64]{3,2,1,0:T(4,128)S(1)}, f32[2,1,4,64]{3,2,1,0:T(4,128)S(1)}, u32[]{:S(2)}, u32[]{:S(2)}) collective-permute-start(f32[2,1,4,64]{3,2,1,0:T(4,128)S(1)} %get-tuple-element.89), channel_id=1, source_target_pairs={{0,4},{4,8},{8,12},{12,16},{16,20},{20,24},{24,28},{1,5},{5,9},{9,... | collective-permute-start | bytes 6152 | tf_op jit(solution)/shard_map/ppermute | solution.py:18
  314.2 5.0 %collective-permute-start.67 = (f32[2,6,1,64]{3,2,1,0:T(1,128)S(1)}, f32[2,6,1,64]{3,2,1,0:T(1,128)S(1)}, u32[]{:S(2)}, u32[]{:S(2)}) collective-permute-start(f32[2,6,1,64]{3,2,1,0:T(1,128)S(1)} %get-tuple-element.81), channel_id=1, source_target_pairs={{0,1},{1,2},{2,3},{4,5},{5,6},{6,7},{8,9},{9,10},{10,11},{12,13},{... | collective-permute-start | bytes 9224 | tf_op jit(solution)/shard_map/ppermute | solution.py:18
  321.5 5.4 %collective-permute-start.69 = (f32[2,1,4,64]{3,2,1,0:T(4,128)S(1)}, f32[2,1,4,64]{3,2,1,0:T(4,128)S(1)}, u32[]{:S(2)}, u32[]{:S(2)}) collective-permute-start(f32[2,1,4,64]{3,2,1,0:T(4,128)S(1)} %get-tuple-element.87), channel_id=1, source_target_pairs={{0,4},{4,8},{8,12},{12,16},{16,20},{20,24},{24,28},{1,5},{5,9},{9,... | collective-permute-start | bytes 6152 | tf_op jit(solution)/shard_map/ppermute | solution.py:18
  329.6 5.0 %collective-permute-start.71 = (f32[2,6,1,64]{3,2,1,0:T(1,128)S(1)}, f32[2,6,1,64]{3,2,1,0:T(1,128)S(1)}, u32[]{:S(2)}, u32[]{:S(2)}) collective-permute-start(f32[2,6,1,64]{3,2,1,0:T(1,128)S(1)} %get-tuple-element.79), channel_id=1, source_target_pairs={{0,1},{1,2},{2,3},{4,5},{5,6},{6,7},{8,9},{9,10},{10,11},{12,13},{... | collective-permute-start | bytes 9224 | tf_op jit(solution)/shard_map/ppermute | solution.py:18
  337.6 5.4 %collective-permute-start.73 = (f32[2,1,8,128]{3,2,1,0:T(8,128)S(1)}, f32[2,1,8,128]{3,2,1,0:T(8,128)S(1)}, u32[]{:S(2)}, u32[]{:S(2)}) collective-permute-start(f32[2,1,8,128]{3,2,1,0:T(8,128)S(1)} %get-tuple-element.67), channel_id=1, source_target_pairs={{0,4},{4,8},{8,12},{12,16},{16,20},{20,24},{24,28},{1,5},{5,9},{9,... | collective-permute-start | bytes 24584 | tf_op jit(solution)/shard_map/ppermute | solution.py:18
  345.8 5.0 %collective-permute-start.75 = (f32[2,10,1,128]{3,0,2,1:T(2,128)S(1)}, f32[2,10,1,128]{3,0,2,1:T(2,128)S(1)}, u32[]{:S(2)}, u32[]{:S(2)}) collective-permute-start(f32[2,10,1,128]{3,0,2,1:T(2,128)S(1)} %copy.412), channel_id=1, source_target_pairs={{0,1},{1,2},{2,3},{4,5},{5,6},{6,7},{8,9},{9,10},{10,11},{12,13},{... | collective-permute-start | bytes 30728 | tf_op jit(solution)/shard_map/ppermute | solution.py:18
  353.3 5.4 %collective-permute-start.77 = (f32[2,1,8,128]{3,2,1,0:T(8,128)S(1)}, f32[2,1,8,128]{3,2,1,0:T(8,128)S(1)}, u32[]{:S(2)}, u32[]{:S(2)}) collective-permute-start(f32[2,1,8,128]{3,2,1,0:T(8,128)S(1)} %get-tuple-element.65), channel_id=1, source_target_pairs={{0,4},{4,8},{8,12},{12,16},{16,20},{20,24},{24,28},{1,5},{5,9},{9,... | collective-permute-start | bytes 24584 | tf_op jit(solution)/shard_map/ppermute | solution.py:18
  361.5 5.0 %collective-permute-start.79 = (f32[2,10,1,128]{3,0,2,1:T(2,128)S(1)}, f32[2,10,1,128]{3,0,2,1:T(2,128)S(1)}, u32[]{:S(2)}, u32[]{:S(2)}) collective-permute-start(f32[2,10,1,128]{3,0,2,1:T(2,128)S(1)} %copy.414), channel_id=1, source_target_pairs={{0,1},{1,2},{2,3},{4,5},{5,6},{6,7},{8,9},{9,10},{10,11},{12,13},{... | collective-permute-start | bytes 30728 | tf_op jit(solution)/shard_map/ppermute | solution.py:18
  377.8 5.6 %collective-permute-start.81 = (f32[2,1,16,256]{3,2,1,0:T(8,128)S(1)}, f32[2,1,16,256]{3,2,1,0:T(8,128)S(1)}, u32[]{:S(2)}, u32[]{:S(2)}) collective-permute-start(f32[2,1,16,256]{3,2,1,0:T(8,128)S(1)} %get-tuple-element.47), channel_id=1, source_target_pairs={{0,4},{4,8},{8,12},{12,16},{16,20},{20,24},{24,28},{1,5},{5,9},{9,... | collective-permute-start | bytes 98312 | tf_op jit(solution)/shard_map/ppermute | solution.py:18
  386.4 5.3 %collective-permute-start.83 = (f32[2,18,1,256]{3,0,2,1:T(2,128)S(1)}, f32[2,18,1,256]{3,0,2,1:T(2,128)S(1)}, u32[]{:S(2)}, u32[]{:S(2)}) collective-permute-start(f32[2,18,1,256]{3,0,2,1:T(2,128)S(1)} %copy.397), channel_id=1, source_target_pairs={{0,1},{1,2},{2,3},{4,5},{5,6},{6,7},{8,9},{9,10},{10,11},{12,13},{... | collective-permute-start | bytes 110600 | tf_op jit(solution)/shard_map/ppermute | solution.py:18
  395.2 5.4 %collective-permute-start.85 = (f32[2,1,16,256]{3,2,1,0:T(8,128)S(1)}, f32[2,1,16,256]{3,2,1,0:T(8,128)S(1)}, u32[]{:S(2)}, u32[]{:S(2)}) collective-permute-start(f32[2,1,16,256]{3,2,1,0:T(8,128)S(1)} %get-tuple-element.45), channel_id=1, source_target_pairs={{0,4},{4,8},{8,12},{12,16},{16,20},{20,24},{24,28},{1,5},{5,9},{9,... | collective-permute-start | bytes 98312 | tf_op jit(solution)/shard_map/ppermute | solution.py:18
  403.7 5.1 %collective-permute-start.87 = (f32[2,18,1,256]{3,0,2,1:T(2,128)S(1)}, f32[2,18,1,256]{3,0,2,1:T(2,128)S(1)}, u32[]{:S(2)}, u32[]{:S(2)}) collective-permute-start(f32[2,18,1,256]{3,0,2,1:T(2,128)S(1)} %copy.403), channel_id=1, source_target_pairs={{0,1},{1,2},{2,3},{4,5},{5,6},{6,7},{8,9},{9,10},{10,11},{12,13},{... | collective-permute-start | bytes 110600 | tf_op jit(solution)/shard_map/ppermute | solution.py:18
  411.9 45.1 %all-reduce.22 = (f32[]{:T(128)}, f32[]{:T(128)}) all-reduce(f32[]{:T(128)} %get-tuple-element.6, f32[]{:T(128)} %get-tuple-element.5), channel_id=1, replica_groups=mesh['wide'=8,'narrow'=4] {'wide','narrow'}, use_global_device_ids=true, to_apply=%region_11.12 | all-reduce | flops 2 | bytes 16 | tf_op jit(solution)/shard_map/psum | solution.py:93
  (335 shorter events, 129.8 us)
Async XLA Ops:
  0.7 41.0 %collective-permute-start = (f32[1,16,256]{2,1,0:T(8,128)S(1)}, f32[1,16,256]{2,1,0:T(8,128)S(1)}, u32[]{:S(2)}, u32[]{:S(2)}) collective-permute-start(f32[1,16,256]{2,1,0:T(8,128)S(1)} %get-tuple-element.56), channel_id=1, source_target_pairs={{4,0},{8,4},{12,8},{16,12},{20,16},{24,20},{28,24},{5,1},{9,5},{13... | collective-permute-start | bytes 49160 | tf_op jit(solution)/shard_map/ppermute | solution.py:21
  2.0 39.0 %collective-permute-start.1 = (f32[1,16,256]{2,1,0:T(8,128)S(1)}, f32[1,16,256]{2,1,0:T(8,128)S(1)}, u32[]{:S(2)}, u32[]{:S(2)}) collective-permute-start(f32[1,16,256]{2,1,0:T(8,128)S(1)} %get-tuple-element.55), channel_id=1, source_target_pairs={{0,4},{4,8},{8,12},{12,16},{16,20},{20,24},{24,28},{1,5},{5,9},{9,... | collective-permute-start | bytes 49160 | tf_op jit(solution)/shard_map/ppermute | solution.py:18
  32.5 32.8 %collective-permute-start.12 = (f32[1,8,128]{2,1,0:T(8,128)S(1)}, f32[1,8,128]{2,1,0:T(8,128)S(1)}, u32[]{:S(2)}, u32[]{:S(2)}) collective-permute-start(f32[1,8,128]{2,1,0:T(8,128)S(1)} %get-tuple-element.76), channel_id=1, source_target_pairs={{4,0},{8,4},{12,8},{16,12},{20,16},{24,20},{28,24},{5,1},{9,5},{13... | collective-permute-start | bytes 12296 | tf_op jit(solution)/shard_map/ppermute | solution.py:21
  33.8 34.8 %collective-permute-start.13 = (f32[1,8,128]{2,1,0:T(8,128)S(1)}, f32[1,8,128]{2,1,0:T(8,128)S(1)}, u32[]{:S(2)}, u32[]{:S(2)}) collective-permute-start(f32[1,8,128]{2,1,0:T(8,128)S(1)} %get-tuple-element.75), channel_id=1, source_target_pairs={{0,4},{4,8},{8,12},{12,16},{16,20},{20,24},{24,28},{1,5},{5,9},{9,... | collective-permute-start | bytes 12296 | tf_op jit(solution)/shard_map/ppermute | solution.py:18
  41.8 8.1 %collective-permute-start.2 = (f32[18,1,256]{2,1,0:T(1,128)S(1)}, f32[18,1,256]{2,1,0:T(1,128)S(1)}, u32[]{:S(2)}, u32[]{:S(2)}) collective-permute-start(f32[18,1,256]{2,1,0:T(1,128)S(1)} %get-tuple-element.54), channel_id=1, source_target_pairs={{1,0},{2,1},{3,2},{5,4},{6,5},{7,6},{9,8},{10,9},{11,10},{13,12},{... | collective-permute-start | bytes 55304 | tf_op jit(solution)/shard_map/ppermute | solution.py:21
  48.3 103.5 %collective-permute-start.24 = (f32[1,4,64]{2,1,0:T(4,128)S(1)}, f32[1,4,64]{2,1,0:T(4,128)S(1)}, u32[]{:S(2)}, u32[]{:S(2)}) collective-permute-start(f32[1,4,64]{2,1,0:T(4,128)S(1)} %get-tuple-element.106), channel_id=1, source_target_pairs={{4,0},{8,4},{12,8},{16,12},{20,16},{24,20},{28,24},{5,1},{9,5},{13... | collective-permute-start | bytes 3080 | tf_op jit(solution)/shard_map/ppermute | solution.py:21
  51.5 7.1 %collective-permute-start.4 = (f32[2,1,16,256]{3,2,1,0:T(8,128)S(1)}, f32[2,1,16,256]{3,2,1,0:T(8,128)S(1)}, u32[]{:S(2)}, u32[]{:S(2)}) collective-permute-start(f32[2,1,16,256]{3,2,1,0:T(8,128)S(1)} %get-tuple-element.52), channel_id=1, source_target_pairs={{4,0},{8,4},{12,8},{16,12},{20,16},{24,20},{28,24},{5,1},{9,5},{13... | collective-permute-start | bytes 98312 | tf_op jit(solution)/shard_map/ppermute | solution.py:21
  52.8 10.1 %collective-permute-start.5 = (f32[2,1,16,256]{3,2,1,0:T(8,128)S(1)}, f32[2,1,16,256]{3,2,1,0:T(8,128)S(1)}, u32[]{:S(2)}, u32[]{:S(2)}) collective-permute-start(f32[2,1,16,256]{3,2,1,0:T(8,128)S(1)} %get-tuple-element.51), channel_id=1, source_target_pairs={{0,4},{4,8},{8,12},{12,16},{16,20},{20,24},{24,28},{1,5},{5,9},{9,... | collective-permute-start | bytes 98312 | tf_op jit(solution)/shard_map/ppermute | solution.py:18
  58.6 98.0 %collective-permute-start.25 = (f32[1,4,64]{2,1,0:T(4,128)S(1)}, f32[1,4,64]{2,1,0:T(4,128)S(1)}, u32[]{:S(2)}, u32[]{:S(2)}) collective-permute-start(f32[1,4,64]{2,1,0:T(4,128)S(1)} %get-tuple-element.105), channel_id=1, source_target_pairs={{0,4},{4,8},{8,12},{12,16},{16,20},{20,24},{24,28},{1,5},{5,9},{9,... | collective-permute-start | bytes 3080 | tf_op jit(solution)/shard_map/ppermute | solution.py:18
  63.0 7.6 %collective-permute-start.6 = (f32[2,18,1,256]{3,0,2,1:T(2,128)S(1)}, f32[2,18,1,256]{3,0,2,1:T(2,128)S(1)}, u32[]{:S(2)}, u32[]{:S(2)}) collective-permute-start(f32[2,18,1,256]{3,0,2,1:T(2,128)S(1)} %copy.351), channel_id=1, source_target_pairs={{1,0},{2,1},{3,2},{5,4},{6,5},{7,6},{9,8},{10,9},{11,10},{13,12},{... | collective-permute-start | bytes 110600 | tf_op jit(solution)/shard_map/ppermute | solution.py:21
  65.3 9.0 %collective-permute-start.7 = (f32[2,18,1,256]{3,0,2,1:T(2,128)S(1)}, f32[2,18,1,256]{3,0,2,1:T(2,128)S(1)}, u32[]{:S(2)}, u32[]{:S(2)}) collective-permute-start(f32[2,18,1,256]{3,0,2,1:T(2,128)S(1)} %copy.353), channel_id=1, source_target_pairs={{0,1},{1,2},{2,3},{4,5},{5,6},{6,7},{8,9},{9,10},{10,11},{12,13},{... | collective-permute-start | bytes 110600 | tf_op jit(solution)/shard_map/ppermute | solution.py:18
  68.6 8.3 %collective-permute-start.14 = (f32[10,1,128]{2,1,0:T(1,128)S(1)}, f32[10,1,128]{2,1,0:T(1,128)S(1)}, u32[]{:S(2)}, u32[]{:S(2)}) collective-permute-start(f32[10,1,128]{2,1,0:T(1,128)S(1)} %get-tuple-element.74), channel_id=1, source_target_pairs={{1,0},{2,1},{3,2},{5,4},{6,5},{7,6},{9,8},{10,9},{11,10},{13,12},{... | collective-permute-start | bytes 15368 | tf_op jit(solution)/shard_map/ppermute | solution.py:21
  70.6 10.4 %collective-permute-start.15 = (f32[10,1,128]{2,1,0:T(1,128)S(1)}, f32[10,1,128]{2,1,0:T(1,128)S(1)}, u32[]{:S(2)}, u32[]{:S(2)}) collective-permute-start(f32[10,1,128]{2,1,0:T(1,128)S(1)} %get-tuple-element.73), channel_id=1, source_target_pairs={{0,1},{1,2},{2,3},{4,5},{5,6},{6,7},{8,9},{9,10},{10,11},{12,13},{... | collective-permute-start | bytes 15368 | tf_op jit(solution)/shard_map/ppermute | solution.py:18
  137.1 7.5 %collective-permute-start.16 = (f32[2,1,8,128]{3,2,1,0:T(8,128)S(1)}, f32[2,1,8,128]{3,2,1,0:T(8,128)S(1)}, u32[]{:S(2)}, u32[]{:S(2)}) collective-permute-start(f32[2,1,8,128]{3,2,1,0:T(8,128)S(1)} %get-tuple-element.72), channel_id=1, source_target_pairs={{4,0},{8,4},{12,8},{16,12},{20,16},{24,20},{28,24},{5,1},{9,5},{13... | collective-permute-start | bytes 24584 | tf_op jit(solution)/shard_map/ppermute | solution.py:21
  138.4 11.4 %collective-permute-start.17 = (f32[2,1,8,128]{3,2,1,0:T(8,128)S(1)}, f32[2,1,8,128]{3,2,1,0:T(8,128)S(1)}, u32[]{:S(2)}, u32[]{:S(2)}) collective-permute-start(f32[2,1,8,128]{3,2,1,0:T(8,128)S(1)} %get-tuple-element.71), channel_id=1, source_target_pairs={{0,4},{4,8},{8,12},{12,16},{16,20},{20,24},{24,28},{1,5},{5,9},{9,... | collective-permute-start | bytes 24584 | tf_op jit(solution)/shard_map/ppermute | solution.py:18
  143.3 47.9 %collective-permute-start.36 = (f32[1,2,32]{2,1,0:T(2,128)S(1)}, f32[1,2,32]{2,1,0:T(2,128)S(1)}, u32[]{:S(2)}, u32[]{:S(2)}) collective-permute-start(f32[1,2,32]{2,1,0:T(2,128)S(1)} %get-tuple-element.126), channel_id=1, source_target_pairs={{4,0},{8,4},{12,8},{16,12},{20,16},{24,20},{28,24},{5,1},{9,5},{13... | collective-permute-start | bytes 776 | tf_op jit(solution)/shard_map/ppermute | solution.py:21
  144.6 46.6 %collective-permute-start.37 = (f32[1,2,32]{2,1,0:T(2,128)S(1)}, f32[1,2,32]{2,1,0:T(2,128)S(1)}, u32[]{:S(2)}, u32[]{:S(2)}) collective-permute-start(f32[1,2,32]{2,1,0:T(2,128)S(1)} %get-tuple-element.125), channel_id=1, source_target_pairs={{0,4},{4,8},{8,12},{12,16},{16,20},{20,24},{24,28},{1,5},{5,9},{9,... | collective-permute-start | bytes 776 | tf_op jit(solution)/shard_map/ppermute | solution.py:18
  149.9 8.7 %collective-permute-start.18 = (f32[2,10,1,128]{3,0,2,1:T(2,128)S(1)}, f32[2,10,1,128]{3,0,2,1:T(2,128)S(1)}, u32[]{:S(2)}, u32[]{:S(2)}) collective-permute-start(f32[2,10,1,128]{3,0,2,1:T(2,128)S(1)} %copy.407), channel_id=1, source_target_pairs={{1,0},{2,1},{3,2},{5,4},{6,5},{7,6},{9,8},{10,9},{11,10},{13,12},{... | collective-permute-start | bytes 30728 | tf_op jit(solution)/shard_map/ppermute | solution.py:21
  151.8 10.4 %collective-permute-start.19 = (f32[2,10,1,128]{3,0,2,1:T(2,128)S(1)}, f32[2,10,1,128]{3,0,2,1:T(2,128)S(1)}, u32[]{:S(2)}, u32[]{:S(2)}) collective-permute-start(f32[2,10,1,128]{3,0,2,1:T(2,128)S(1)} %copy.408), channel_id=1, source_target_pairs={{0,1},{1,2},{2,3},{4,5},{5,6},{6,7},{8,9},{9,10},{10,11},{12,13},{... | collective-permute-start | bytes 30728 | tf_op jit(solution)/shard_map/ppermute | solution.py:18
  156.6 7.5 %collective-permute-start.26 = (f32[6,1,64]{2,1,0:T(1,128)S(1)}, f32[6,1,64]{2,1,0:T(1,128)S(1)}, u32[]{:S(2)}, u32[]{:S(2)}) collective-permute-start(f32[6,1,64]{2,1,0:T(1,128)S(1)} %get-tuple-element.96), channel_id=1, source_target_pairs={{1,0},{2,1},{3,2},{5,4},{6,5},{7,6},{9,8},{10,9},{11,10},{13,12},{... | collective-permute-start | bytes 4616 | tf_op jit(solution)/shard_map/ppermute | solution.py:21
  158.6 10.7 %collective-permute-start.27 = (f32[6,1,64]{2,1,0:T(1,128)S(1)}, f32[6,1,64]{2,1,0:T(1,128)S(1)}, u32[]{:S(2)}, u32[]{:S(2)}) collective-permute-start(f32[6,1,64]{2,1,0:T(1,128)S(1)} %get-tuple-element.95), channel_id=1, source_target_pairs={{0,1},{1,2},{2,3},{4,5},{5,6},{6,7},{8,9},{9,10},{10,11},{12,13},{... | collective-permute-start | bytes 4616 | tf_op jit(solution)/shard_map/ppermute | solution.py:18
  162.6 6.8 %collective-permute-start.20 = (f32[2,1,8,128]{3,2,1,0:T(8,128)S(1)}, f32[2,1,8,128]{3,2,1,0:T(8,128)S(1)}, u32[]{:S(2)}, u32[]{:S(2)}) collective-permute-start(f32[2,1,8,128]{3,2,1,0:T(8,128)S(1)} %get-tuple-element.70), channel_id=1, source_target_pairs={{4,0},{8,4},{12,8},{16,12},{20,16},{24,20},{28,24},{5,1},{9,5},{13... | collective-permute-start | bytes 24584 | tf_op jit(solution)/shard_map/ppermute | solution.py:21
  191.9 12.6 %collective-permute-start.30 = (f32[2,6,1,64]{3,2,1,0:T(1,128)S(1)}, f32[2,6,1,64]{3,2,1,0:T(1,128)S(1)}, u32[]{:S(2)}, u32[]{:S(2)}) collective-permute-start(f32[2,6,1,64]{3,2,1,0:T(1,128)S(1)} %get-tuple-element.86), channel_id=1, source_target_pairs={{1,0},{2,1},{3,2},{5,4},{6,5},{7,6},{9,8},{10,9},{11,10},{13,12},{... | collective-permute-start | bytes 9224 | tf_op jit(solution)/shard_map/ppermute | solution.py:21
  193.9 10.7 %collective-permute-start.31 = (f32[2,6,1,64]{3,2,1,0:T(1,128)S(1)}, f32[2,6,1,64]{3,2,1,0:T(1,128)S(1)}, u32[]{:S(2)}, u32[]{:S(2)}) collective-permute-start(f32[2,6,1,64]{3,2,1,0:T(1,128)S(1)} %get-tuple-element.85), channel_id=1, source_target_pairs={{0,1},{1,2},{2,3},{4,5},{5,6},{6,7},{8,9},{9,10},{10,11},{12,13},{... | collective-permute-start | bytes 9224 | tf_op jit(solution)/shard_map/ppermute | solution.py:18
  198.9 12.3 %collective-permute-start.38 = (f32[4,1,32]{2,1,0:T(1,128)S(1)}, f32[4,1,32]{2,1,0:T(1,128)S(1)}, u32[]{:S(2)}, u32[]{:S(2)}) collective-permute-start(f32[4,1,32]{2,1,0:T(1,128)S(1)} %get-tuple-element.121), channel_id=1, source_target_pairs={{1,0},{2,1},{3,2},{5,4},{6,5},{7,6},{9,8},{10,9},{11,10},{13,12},{... | collective-permute-start | bytes 1544 | tf_op jit(solution)/shard_map/ppermute | solution.py:21
  200.9 10.4 %collective-permute-start.39 = (f32[4,1,32]{2,1,0:T(1,128)S(1)}, f32[4,1,32]{2,1,0:T(1,128)S(1)}, u32[]{:S(2)}, u32[]{:S(2)}) collective-permute-start(f32[4,1,32]{2,1,0:T(1,128)S(1)} %get-tuple-element.120), channel_id=1, source_target_pairs={{0,1},{1,2},{2,3},{4,5},{5,6},{6,7},{8,9},{9,10},{10,11},{12,13},{... | collective-permute-start | bytes 1544 | tf_op jit(solution)/shard_map/ppermute | solution.py:18
  219.2 13.2 %collective-permute-start.40 = (f32[2,1,2,32]{3,2,1,0:T(2,128)S(1)}, f32[2,1,2,32]{3,2,1,0:T(2,128)S(1)}, u32[]{:S(2)}, u32[]{:S(2)}) collective-permute-start(f32[2,1,2,32]{3,2,1,0:T(2,128)S(1)} %get-tuple-element.119), channel_id=1, source_target_pairs={{4,0},{8,4},{12,8},{16,12},{20,16},{24,20},{28,24},{5,1},{9,5},{13... | collective-permute-start | bytes 1544 | tf_op jit(solution)/shard_map/ppermute | solution.py:21
  220.5 11.9 %collective-permute-start.41 = (f32[2,1,2,32]{3,2,1,0:T(2,128)S(1)}, f32[2,1,2,32]{3,2,1,0:T(2,128)S(1)}, u32[]{:S(2)}, u32[]{:S(2)}) collective-permute-start(f32[2,1,2,32]{3,2,1,0:T(2,128)S(1)} %get-tuple-element.118), channel_id=1, source_target_pairs={{0,4},{4,8},{8,12},{12,16},{16,20},{20,24},{24,28},{1,5},{5,9},{9,... | collective-permute-start | bytes 1544 | tf_op jit(solution)/shard_map/ppermute | solution.py:18
  226.0 13.2 %collective-permute-start.48 = (f32[1,1,16]{2,1,0:T(1,128)S(1)}, f32[1,1,16]{2,1,0:T(1,128)S(1)}, u32[]{:S(2)}, u32[]{:S(2)}) collective-permute-start(f32[1,1,16]{2,1,0:T(1,128)S(1)} %multiply_bitcast_fusion), channel_id=1, source_target_pairs={{4,0},{8,4},{12,8},{16,12},{20,16},{24,20},{28,24},{5,1},{9,5},{13... | collective-permute-start | bytes 200 | tf_op jit(solution)/shard_map/ppermute | solution.py:21
  227.3 11.9 %collective-permute-start.49 = (f32[1,1,16]{2,1,0:T(1,128)S(1)}, f32[1,1,16]{2,1,0:T(1,128)S(1)}, u32[]{:S(2)}, u32[]{:S(2)}) collective-permute-start(f32[1,1,16]{2,1,0:T(1,128)S(1)} %multiply_bitcast_fusion), channel_id=1, source_target_pairs={{0,4},{4,8},{8,12},{12,16},{16,20},{20,24},{24,28},{1,5},{5,9},{9,... | collective-permute-start | bytes 200 | tf_op jit(solution)/shard_map/ppermute | solution.py:18
  232.5 12.3 %collective-permute-start.42 = (f32[2,4,1,32]{3,2,1,0:T(1,128)S(1)}, f32[2,4,1,32]{3,2,1,0:T(1,128)S(1)}, u32[]{:S(2)}, u32[]{:S(2)}) collective-permute-start(f32[2,4,1,32]{3,2,1,0:T(1,128)S(1)} %get-tuple-element.104), channel_id=1, source_target_pairs={{1,0},{2,1},{3,2},{5,4},{6,5},{7,6},{9,8},{10,9},{11,10},{13,12},{... | collective-permute-start | bytes 3080 | tf_op jit(solution)/shard_map/ppermute | solution.py:21
  234.4 10.4 %collective-permute-start.43 = (f32[2,4,1,32]{3,2,1,0:T(1,128)S(1)}, f32[2,4,1,32]{3,2,1,0:T(1,128)S(1)}, u32[]{:S(2)}, u32[]{:S(2)}) collective-permute-start(f32[2,4,1,32]{3,2,1,0:T(1,128)S(1)} %get-tuple-element.103), channel_id=1, source_target_pairs={{0,1},{1,2},{2,3},{4,5},{5,6},{6,7},{8,9},{9,10},{10,11},{12,13},{... | collective-permute-start | bytes 3080 | tf_op jit(solution)/shard_map/ppermute | solution.py:18
  239.2 12.3 %collective-permute-start.50 = (f32[3,1,16]{2,1,0:T(1,128)S(1)}, f32[3,1,16]{2,1,0:T(1,128)S(1)}, u32[]{:S(2)}, u32[]{:S(2)}) collective-permute-start(f32[3,1,16]{2,1,0:T(1,128)S(1)} %pad_maximum_fusion.205), channel_id=1, source_target_pairs={{1,0},{2,1},{3,2},{5,4},{6,5},{7,6},{9,8},{10,9},{11,10},{13,12},{... | collective-permute-start | bytes 584 | tf_op jit(solution)/shard_map/ppermute | solution.py:21
  241.2 10.3 %collective-permute-start.51 = (f32[3,1,16]{2,1,0:T(1,128)S(1)}, f32[3,1,16]{2,1,0:T(1,128)S(1)}, u32[]{:S(2)}, u32[]{:S(2)}) collective-permute-start(f32[3,1,16]{2,1,0:T(1,128)S(1)} %pad_maximum_fusion.205), channel_id=1, source_target_pairs={{0,1},{1,2},{2,3},{4,5},{5,6},{6,7},{8,9},{9,10},{10,11},{12,13},{... | collective-permute-start | bytes 584 | tf_op jit(solution)/shard_map/ppermute | solution.py:18
  265.8 7.0 %collective-permute-start.54 = (f32[2,3,1,16]{3,0,2,1:T(2,128)S(1)}, f32[2,3,1,16]{3,0,2,1:T(2,128)S(1)}, u32[]{:S(2)}, u32[]{:S(2)}) collective-permute-start(f32[2,3,1,16]{3,0,2,1:T(2,128)S(1)} %pad_maximum_fusion.196), channel_id=1, source_target_pairs={{1,0},{2,1},{3,2},{5,4},{6,5},{7,6},{9,8},{10,9},{11,10},{13,12},{... | collective-permute-start | bytes 1160 | tf_op jit(solution)/shard_map/ppermute | solution.py:21
  281.1 7.0 %collective-permute-start.58 = (f32[2,4,1,32]{3,2,1,0:T(1,128)S(1)}, f32[2,4,1,32]{3,2,1,0:T(1,128)S(1)}, u32[]{:S(2)}, u32[]{:S(2)}) collective-permute-start(f32[2,4,1,32]{3,2,1,0:T(1,128)S(1)} %get-tuple-element.100), channel_id=1, source_target_pairs={{1,0},{2,1},{3,2},{5,4},{6,5},{7,6},{9,8},{10,9},{11,10},{13,12},{... | collective-permute-start | bytes 3080 | tf_op jit(solution)/shard_map/ppermute | solution.py:21
  296.4 7.0 %collective-permute-start.62 = (f32[2,4,1,32]{3,2,1,0:T(1,128)S(1)}, f32[2,4,1,32]{3,2,1,0:T(1,128)S(1)}, u32[]{:S(2)}, u32[]{:S(2)}) collective-permute-start(f32[2,4,1,32]{3,2,1,0:T(1,128)S(1)} %get-tuple-element.98), channel_id=1, source_target_pairs={{1,0},{2,1},{3,2},{5,4},{6,5},{7,6},{9,8},{10,9},{11,10},{13,12},{... | collective-permute-start | bytes 3080 | tf_op jit(solution)/shard_map/ppermute | solution.py:21
  304.7 6.7 %collective-permute-start.64 = (f32[2,1,4,64]{3,2,1,0:T(4,128)S(1)}, f32[2,1,4,64]{3,2,1,0:T(4,128)S(1)}, u32[]{:S(2)}, u32[]{:S(2)}) collective-permute-start(f32[2,1,4,64]{3,2,1,0:T(4,128)S(1)} %get-tuple-element.90), channel_id=1, source_target_pairs={{4,0},{8,4},{12,8},{16,12},{20,16},{24,20},{28,24},{5,1},{9,5},{13... | collective-permute-start | bytes 6152 | tf_op jit(solution)/shard_map/ppermute | solution.py:21
  312.2 7.0 %collective-permute-start.66 = (f32[2,6,1,64]{3,2,1,0:T(1,128)S(1)}, f32[2,6,1,64]{3,2,1,0:T(1,128)S(1)}, u32[]{:S(2)}, u32[]{:S(2)}) collective-permute-start(f32[2,6,1,64]{3,2,1,0:T(1,128)S(1)} %get-tuple-element.82), channel_id=1, source_target_pairs={{1,0},{2,1},{3,2},{5,4},{6,5},{7,6},{9,8},{10,9},{11,10},{13,12},{... | collective-permute-start | bytes 9224 | tf_op jit(solution)/shard_map/ppermute | solution.py:21
  327.7 7.0 %collective-permute-start.70 = (f32[2,6,1,64]{3,2,1,0:T(1,128)S(1)}, f32[2,6,1,64]{3,2,1,0:T(1,128)S(1)}, u32[]{:S(2)}, u32[]{:S(2)}) collective-permute-start(f32[2,6,1,64]{3,2,1,0:T(1,128)S(1)} %get-tuple-element.80), channel_id=1, source_target_pairs={{1,0},{2,1},{3,2},{5,4},{6,5},{7,6},{9,8},{10,9},{11,10},{13,12},{... | collective-permute-start | bytes 9224 | tf_op jit(solution)/shard_map/ppermute | solution.py:21
  336.3 6.7 %collective-permute-start.72 = (f32[2,1,8,128]{3,2,1,0:T(8,128)S(1)}, f32[2,1,8,128]{3,2,1,0:T(8,128)S(1)}, u32[]{:S(2)}, u32[]{:S(2)}) collective-permute-start(f32[2,1,8,128]{3,2,1,0:T(8,128)S(1)} %get-tuple-element.68), channel_id=1, source_target_pairs={{4,0},{8,4},{12,8},{16,12},{20,16},{24,20},{28,24},{5,1},{9,5},{13... | collective-permute-start | bytes 24584 | tf_op jit(solution)/shard_map/ppermute | solution.py:21
  343.9 7.0 %collective-permute-start.74 = (f32[2,10,1,128]{3,0,2,1:T(2,128)S(1)}, f32[2,10,1,128]{3,0,2,1:T(2,128)S(1)}, u32[]{:S(2)}, u32[]{:S(2)}) collective-permute-start(f32[2,10,1,128]{3,0,2,1:T(2,128)S(1)} %copy.411), channel_id=1, source_target_pairs={{1,0},{2,1},{3,2},{5,4},{6,5},{7,6},{9,8},{10,9},{11,10},{13,12},{... | collective-permute-start | bytes 30728 | tf_op jit(solution)/shard_map/ppermute | solution.py:21
  352.0 6.7 %collective-permute-start.76 = (f32[2,1,8,128]{3,2,1,0:T(8,128)S(1)}, f32[2,1,8,128]{3,2,1,0:T(8,128)S(1)}, u32[]{:S(2)}, u32[]{:S(2)}) collective-permute-start(f32[2,1,8,128]{3,2,1,0:T(8,128)S(1)} %get-tuple-element.66), channel_id=1, source_target_pairs={{4,0},{8,4},{12,8},{16,12},{20,16},{24,20},{28,24},{5,1},{9,5},{13... | collective-permute-start | bytes 24584 | tf_op jit(solution)/shard_map/ppermute | solution.py:21
  359.6 7.0 %collective-permute-start.78 = (f32[2,10,1,128]{3,0,2,1:T(2,128)S(1)}, f32[2,10,1,128]{3,0,2,1:T(2,128)S(1)}, u32[]{:S(2)}, u32[]{:S(2)}) collective-permute-start(f32[2,10,1,128]{3,0,2,1:T(2,128)S(1)} %copy.413), channel_id=1, source_target_pairs={{1,0},{2,1},{3,2},{5,4},{6,5},{7,6},{9,8},{10,9},{11,10},{13,12},{... | collective-permute-start | bytes 30728 | tf_op jit(solution)/shard_map/ppermute | solution.py:21
  376.4 6.9 %collective-permute-start.80 = (f32[2,1,16,256]{3,2,1,0:T(8,128)S(1)}, f32[2,1,16,256]{3,2,1,0:T(8,128)S(1)}, u32[]{:S(2)}, u32[]{:S(2)}) collective-permute-start(f32[2,1,16,256]{3,2,1,0:T(8,128)S(1)} %get-tuple-element.48), channel_id=1, source_target_pairs={{4,0},{8,4},{12,8},{16,12},{20,16},{24,20},{28,24},{5,1},{9,5},{13... | collective-permute-start | bytes 98312 | tf_op jit(solution)/shard_map/ppermute | solution.py:21
  384.4 7.2 %collective-permute-start.82 = (f32[2,18,1,256]{3,0,2,1:T(2,128)S(1)}, f32[2,18,1,256]{3,0,2,1:T(2,128)S(1)}, u32[]{:S(2)}, u32[]{:S(2)}) collective-permute-start(f32[2,18,1,256]{3,0,2,1:T(2,128)S(1)} %copy.395), channel_id=1, source_target_pairs={{1,0},{2,1},{3,2},{5,4},{6,5},{7,6},{9,8},{10,9},{11,10},{13,12},{... | collective-permute-start | bytes 110600 | tf_op jit(solution)/shard_map/ppermute | solution.py:21
  393.9 6.7 %collective-permute-start.84 = (f32[2,1,16,256]{3,2,1,0:T(8,128)S(1)}, f32[2,1,16,256]{3,2,1,0:T(8,128)S(1)}, u32[]{:S(2)}, u32[]{:S(2)}) collective-permute-start(f32[2,1,16,256]{3,2,1,0:T(8,128)S(1)} %get-tuple-element.46), channel_id=1, source_target_pairs={{4,0},{8,4},{12,8},{16,12},{20,16},{24,20},{28,24},{5,1},{9,5},{13... | collective-permute-start | bytes 98312 | tf_op jit(solution)/shard_map/ppermute | solution.py:21
  401.7 7.1 %collective-permute-start.86 = (f32[2,18,1,256]{3,0,2,1:T(2,128)S(1)}, f32[2,18,1,256]{3,0,2,1:T(2,128)S(1)}, u32[]{:S(2)}, u32[]{:S(2)}) collective-permute-start(f32[2,18,1,256]{3,0,2,1:T(2,128)S(1)} %copy.401), channel_id=1, source_target_pairs={{1,0},{2,1},{3,2},{5,4},{6,5},{7,6},{9,8},{10,9},{11,10},{13,12},{... | collective-permute-start | bytes 110600 | tf_op jit(solution)/shard_map/ppermute | solution.py:21
  (55 other events, 561.7 us)
where the time goes:
time: 463 us; the launch traced here: 459 us
  starting transfers between devices  281 us (61%)
  local copies, waits for them, and re-layouts  74.9 us (16%)
  blocking collectives  45.1 us (10%)
  other arithmetic  34.1 us (7%)
  waiting for transfers between devices  20.2 us (4%)
    ppermute x44, starting transfers between devices, with_halo(): lax.ppermute(lax.slice_in_dim(block, block.shape[dim] - width, None, axis...  208 us
    ppermute x44, starting transfers between devices, with_halo(): lax.ppermute(lax.slice_in_dim(block, 0, width, axis=dim), axis, backward)  72.7 us
    psum x1, blocking collectives, inner_sums(): lax.psum((jnp.sum(adjoint_b * cotangent), jnp.sum(sav_vector * adjoint_b)...  45.1 us
    reshape x3, local copies, waits for them, and re-layouts, coarsen(): values.reshape(count, size_x // 2, 2, size_y // 2, 2, size_z // 2, 2)  40.9 us
    reduce_sum x9, other arithmetic, coarsen(): return blocks.mean(axis=(2, 4, 6))  22.5 us
    ppermute x44, waiting for transfers between devices, with_halo(): lax.ppermute(lax.slice_in_dim(block, block.shape[dim] - width, None, axis...  20.1 us
    another operation x1, local copies, waits for them, and re-layouts, coarsen(): values.reshape(count, size_x // 2, 2, size_y // 2, 2, size_z // 2, 2)  18.9 us
  transfers between devices with their start and end apart: 88, of which 27 were waited for; matrix products, arithmetic and copies ran while one was open for 20% of the time, Pallas kernels for 0%

commit v1 on v0

v1 whole, which is shorter than its diff:
```python
import functools
import jax
import jax.numpy as jnp
from jax import lax
from jax.experimental import pallas as pl
from jax.experimental.pallas import tpu as pltpu
from jax.sharding import PartitionSpec as P

DAMPING = 0.8
KEEP = 1.0 - DAMPING
BASE_TAU = 16.0
H0 = 4
H1 = 5
PAD = 2
MESH = pl.DeviceIdType.MESH
F32 = jnp.float32
SIDES = [(-1, 0), (1, 0), (0, -1), (0, 1), (-1, -1), (-1, 1), (1, -1), (1, 1)]
OPPOSITE = [1, 0, 3, 2, 7, 6, 5, 4]


def iota(shape, dim):
    return lax.broadcasted_iota(jnp.int32, shape, dim)


def shift(value, amount, axis):
    return pltpu.roll(value, amount % value.shape[axis], axis)


def squeeze_matrix(rows, cols, offset=0):
    i, j = iota((rows, cols), 0), iota((rows, cols), 1)
    k = i - 2 * (j - offset)
    return jnp.where((k == 0) | (k == 1), 1.0, 0.0).astype(F32)


def spread_matrix(rows, cols):
    i, j = iota((rows, cols), 0), iota((rows, cols), 1)
    k = j - 2 * i
    return jnp.where((k == 0) | (k == 1), 1.0, 0.0).astype(F32)


def mm(a, b):
    return jnp.dot(a, b, precision=lax.Precision.HIGHEST, preferred_element_type=F32)


def rounded(x):
    return x.astype(jnp.bfloat16).astype(F32)


def slabs(lo, hi, chunk, body):
    def step(i, _):
        for k in range(chunk):
            body(lo + i * chunk + k)
        return 0

    lax.fori_loop(0, (hi - lo) // chunk, step, 0)


def build(m, cx, cy, cz, rd, d, lo, hi, tau, seg, chunk):
    shape = m.shape[1:]
    row = iota(shape, 0)
    lane = lax.rem(iota(shape, 1), seg)
    last_row, first_row = row == shape[0] - 1, row == 0
    last_lane, first_lane = lane == seg - 1, lane == 0
    half = 0.5 * tau

    def body(a):
        own = m[a]
        xp, xm = m[a + 1], m[a - 1]
        yp = jnp.where(last_row, 0.0, shift(own, -1, 0))
        ym = jnp.where(first_row, 0.0, shift(own, 1, 0))
        zp = jnp.where(last_lane, 0.0, shift(own, -1, 1))
        zm = jnp.where(first_lane, 0.0, shift(own, 1, 1))
        total = 1.0
        for other, ref in ((xp, cx), (xm, None), (yp, cy), (ym, None), (zp, cz), (zm, None)):
            face = rounded(half * (own + other))
            total = total + face
            if ref is not None:
                ref[a] = jnp.where(jnp.minimum(own, other) > 0.0, face, 0.0)
        rd[a] = DAMPING / total
        if d is not None:
            d[a] = total

    slabs(lo, hi, chunk, body)


def neighbours(v, a, cx, cy, cz):
    own = v[a]
    cya, cza = cy[a], cz[a]
    total = cx[a] * v[a + 1] + cx[a - 1] * v[a - 1]
    total = total + (cya * shift(own, -1, 0) + shift(cya * own, 1, 0))
    total = total + (cza * shift(own, -1, 1) + shift(cza * own, 1, 1))
    return own, total


def sweep(vin, vout, r, ops, lo, hi, chunk):
    cx, cy, cz, rd, d = ops

    def body(a):
        for vi, vo, ri in zip(vin, vout, r):
            own, t = neighbours(vi, a, cx, cy, cz)
            vo[a] = KEEP * own + rd[a] * (ri[a] + t)

    slabs(lo, hi, chunk, body)


def residual(vi, ri, a, ops):
    cx, cy, cz, rd, d = ops
    own, t = neighbours(vi, a, cx, cy, cz)
    diag = d[a] if d is not None else DAMPING / rd[a]
    return own, ri[a] + t - diag * own


def fold(x):
    total = None
    for i in range(x.shape[0] // 8):
        for j in range(x.shape[1] // 128):
            part = x[8 * i : 8 * i + 8, 128 * j : 128 * j + 128]
            total = part if total is None else total + part
    return total


def kernel(nw, nn, bx, by, nz, m_ref, s_ref, c_ref, out_ref,
           m0, cx0, cy0, cz0, rd0, d0, rs0, rc0, us0, uc0, vs0, vc0,
           rx, yp, ry, cp, rcn,
           m1, cx1, cy1, cz1, rd1, d1, r1, u1, v1, w1,
           cx2, cy2, cz2, rd2, r2, u2, v2,
           cx3, cy3, cz3, rd3, r3, u3, v3,
           cx4, cy4, cz4, rd4, r4, u4, v4,
           t0, t0y, t1, t1y, sm2, sr2, sp2, gm, gr, gp, pb, pbs, t2, t2y, f1, f1p, f0a, f0b,
           e0s, e0r, m1s, m1r, e1s, e1r,
           ams, amr, bms, bmr, ars, arr, aps, apr, brs, brr, bps, bpr):
    iw, ino = lax.axis_index("wide"), lax.axis_index("narrow")
    b1x, b1y, z1 = bx // 2, by // 2, nz // 2
    b2x, b2y, z2 = bx // 4, by // 4, nz // 4
    x2, x3, x4 = nw * b2x, nw * b2x // 2, nw * b2x // 4
    xs0 = bx + 2 * H0
    there = []
    for dx, dy in SIDES:
        ok = None
        for cond, on in ((iw > 0, dx < 0), (iw < nw - 1, dx > 0), (ino > 0, dy < 0), (ino < nn - 1, dy > 0)):
            if on:
                ok = cond if ok is None else jnp.logical_and(ok, cond)
        there.append(ok)

    def peer(side):
        return (iw + SIDES[side][0], ino + SIDES[side][1])

    barrier = pltpu.get_barrier_semaphore()

    def greet(j, _):
        pl.semaphore_signal(barrier, inc=1, device_id=(lax.rem(iw + j, nw), ino), device_id_type=MESH)
        return 0

    lax.fori_loop(1, nw, greet, 0)
    for j in range(1, nn):
        pl.semaphore_signal(barrier, inc=1, device_id=(iw, lax.rem(ino + j, nn)), device_id_type=MESH)
    for k in range(4, 8):
        @pl.when(there[k])
        def _():
            pl.semaphore_signal(barrier, inc=1, device_id=peer(k), device_id_type=MESH)

    for side, (m_lo, r_lo) in enumerate(((0, 0), (by - 4, by - 3))):
        for k in range(4):
            yp[side, k] = m_ref[:, m_lo + k, :]
        for k in range(3):
            yp[side, 4 + k] = s_ref[:, r_lo + k, :]
            yp[side, 7 + k] = c_ref[:, r_lo + k, :]
    for k in range(4, 8):
        dx, dy = SIDES[k]
        m_x, m_y = (0 if dx < 0 else bx - 3), (0 if dy < 0 else by - 3)
        r_x, r_y = (0 if dx < 0 else bx - 2), (0 if dy < 0 else by - 2)
        for i in range(3):
            cp[k - 4, 3 * i : 3 * i + 3, :] = m_ref[m_x + i, m_y : m_y + 3, :]
        for i in range(2):
            cp[k - 4, 9 + 2 * i : 11 + 2 * i, :] = s_ref[r_x + i, r_y : r_y + 2, :]
            cp[k - 4, 13 + 2 * i : 15 + 2 * i, :] = c_ref[r_x + i, r_y : r_y + 2, :]

    beside_x = jnp.minimum(iw, 1) + jnp.minimum(nw - 1 - iw, 1)
    beside_y = jnp.minimum(ino, 1) + jnp.minimum(nn - 1 - ino, 1)
    pl.semaphore_wait(barrier, nw + nn - 2 + beside_x * beside_y)

    def remote(src, dst, ssem, rsem, dev):
        return pltpu.make_async_remote_copy(src_ref=src, dst_ref=dst, send_sem=ssem, recv_sem=rsem,
                                            device_id=dev, device_id_type=MESH)

    def e0_copies(side, recv):
        other = OPPOSITE[side]
        land = side if recv else other
        dev = peer(side)
        if side < 2:
            out = []
            at = 0
            for n, (ref, width) in enumerate(((m_ref, 4), (s_ref, 3), (c_ref, 3))):
                lo = 0 if side == 0 else bx - width
                out.append(remote(ref.at[lo : lo + width], rx.at[land, at : at + width],
                                  e0s.at[side, n], e0r.at[land, n], dev))
                at += width
            return out
        if side < 4:
            return [remote(yp.at[side - 2], ry.at[land - 2], e0s.at[side, 0], e0r.at[land, 0], dev)]
        return [remote(cp.at[side - 4], rcn.at[land - 4], e0s.at[side, 0], e0r.at[land, 0], dev)]

    def box1(side, sending, width):
        dx, dy = SIDES[side]
        own = H1
        if sending:
            xlo, w = (own, width) if dx < 0 else ((own + b1x - width, width) if dx > 0 else (own, b1x))
            ylo = b1y
        else:
            xlo, w = (own - width, width) if dx < 0 else ((own + b1x, width) if dx > 0 else (own, b1x))
            ylo = b1y * (1 + dy)
        return xlo, w, ylo

    def level1_copies(ref, ssem, rsem, side, recv, width):
        land = side if recv else OPPOSITE[side]
        sx, w, sy = box1(side, True, width)
        tx, _, ty = box1(land, False, width)
        return [remote(ref.at[v, sx : sx + w, sy : sy + b1y], ref.at[v, tx : tx + w, ty : ty + b1y],
                       ssem.at[side, v], rsem.at[land, v], peer(side)) for v in range(ref.shape[0])]

    def each(fn, act):
        for side in range(8):
            @pl.when(there[side])
            def _():
                for copy in fn(side):
                    act(copy)

    def start(copy):
        copy.start()

    each(lambda k: e0_copies(k, False), start)

    zc0 = squeeze_matrix(nz, z1)
    zc1 = squeeze_matrix(z1, z1)
    zc1b = squeeze_matrix(z1, z1, z2)
    zr = spread_matrix(z1, z1)

    def pair_rows(flat, half_rows):
        return flat[pl.ds(0, half_rows, stride=2), :] + flat[pl.ds(1, half_rows, stride=2), :]

    for i in range(b1x):
        t0[0, i * by : (i + 1) * by, :] = m_ref[2 * i] + m_ref[2 * i + 1]
    t0y[...] = mm(t0[0], zc0)
    mob1 = 0.125 * pair_rows(t0y, b1x * b1y)
    for i in range(b1x):
        m1[0, H1 + i, b1y : 2 * b1y, :] = mob1[i * b1y : (i + 1) * b1y]

    def clear1(ref, width):
        for side in range(8):
            xlo, w, ylo = box1(side, False, width)
            @pl.when(jnp.logical_not(there[side]))
            def _():
                ref[:, xlo : xlo + w, ylo : ylo + b1y, :] = jnp.zeros((ref.shape[0], w, b1y, z1), F32)

    clear1(m1, 5)
    clear1(r1, 4)
    each(lambda k: level1_copies(m1, m1s, m1r, k, False, 5), start)
    for i in range(b2x):
        t1[0, i * b1y : (i + 1) * b1y, :] = mob1[2 * i * b1y : (2 * i + 1) * b1y] + mob1[(2 * i + 1) * b1y : (2 * i + 2) * b1y]
    t1y[...] = mm(t1[0], zc1 + zc1b)
    mob2 = 0.125 * pair_rows(t1y, b2x * b2y)
    sm2[...] = mob2
    gm[ino, iw] = mob2

    def wide_copy(src, dst_ref, ssem, rsem, j, recv):
        to = lax.rem(iw + j, nw)
        if recv:
            return remote(src, dst_ref(to), ssem.at[j], rsem.at[to], (to, ino))
        return remote(src, dst_ref(iw), ssem.at[j], rsem.at[iw], (to, ino))

    def over_wide(src, dst_ref, ssem, rsem, what):
        def step(j, _):
            copy = wide_copy(src, dst_ref, ssem, rsem, j, what == "recv")
            if what == "start":
                copy.start()
            elif what == "recv":
                copy.wait_recv()
            else:
                copy.wait_send()
            return 0

        lax.fori_loop(1, nw, step, 0)

    def over_narrow(src, dst_ref, ssem, rsem, what):
        for j in range(1, nn):
            to = lax.rem(ino + j, nn)
            if what == "recv":
                remote(src, dst_ref(to), ssem.at[j], rsem.at[to], (iw, to)).wait_recv()
            else:
                copy = remote(src, dst_ref(ino), ssem.at[j], rsem.at[ino], (iw, to))
                if what == "start":
                    copy.start()
                else:
                    copy.wait_send()

    gather_m = (sm2, lambda w: gm.at[ino, w], ams, amr)
    spread_m = (gm.at[ino], lambda n: gm.at[n], bms, bmr)
    gather_r = (sr2, lambda w: gr.at[ino, w], ars, arr)
    gather_p = (sp2, lambda w: gp.at[w], aps, apr)
    spread_r = (gr.at[ino], lambda n: gr.at[n], brs, brr)
    spread_p = (pb, lambda n: pbs.at[n], bps, bpr)
    over_wide(*gather_m, "start")

    blank = jnp.zeros((H0, m0.shape[1], nz), F32)
    for ref, src in ((m0, m_ref), (rs0, s_ref), (rc0, c_ref)):
        ref[0:H0] = blank
        ref[H0 + bx :] = blank

        def put(i, _):
            ref[H0 + i, H0 : H0 + by, :] = src[i]
            return 0

        lax.fori_loop(0, bx, put, 0)
    for ref in (u2, v2, u3, v3, u4, v4):
        zero = jnp.zeros(ref.shape[1:], F32)
        for a in (0, 1, ref.shape[0] - 2, ref.shape[0] - 1):
            ref[a] = zero
    for ref in (cx2, cx3, cx4):
        ref[PAD - 1] = jnp.zeros(ref.shape[1:], F32)
    for k in range(2):
        @pl.when(jnp.logical_not(there[k]))
        def _():
            rx[k] = jnp.zeros(rx.shape[1:], F32)

        @pl.when(jnp.logical_not(there[2 + k]))
        def _():
            ry[k] = jnp.zeros(ry.shape[1:], F32)
    for k in range(4):
        @pl.when(jnp.logical_not(there[4 + k]))
        def _():
            rcn[k] = jnp.zeros(rcn.shape[1:], F32)

    each(lambda k: e0_copies(k, True), lambda c: c.wait_recv())
    for k, ref, at, width in ((0, m0, 0, 4), (0, rs0, 4, 3), (0, rc0, 7, 3)):
        for i in range(width):
            ref[H0 - width + i, H0 : H0 + by, :] = rx[0, at + i]
            ref[H0 + bx + i, H0 : H0 + by, :] = rx[1, at + i]
            ref[H0 : H0 + bx, H0 - width + i, :] = ry[0, at + i]
            ref[H0 : H0 + bx, H0 + by + i, :] = ry[1, at + i]
    for k in range(4):
        dx, dy = SIDES[4 + k]
        m_x, m_y = (H0 - 3 if dx < 0 else H0 + bx), (H0 - 3 if dy < 0 else H0 + by)
        r_x, r_y = (H0 - 2 if dx < 0 else H0 + bx), (H0 - 2 if dy < 0 else H0 + by)
        for i in range(3):
            m0[m_x + i, m_y : m_y + 3, :] = rcn[k, 3 * i : 3 * i + 3, :]
        for i in range(2):
            rs0[r_x + i, r_y : r_y + 2, :] = rcn[k, 9 + 2 * i : 11 + 2 * i, :]
            rc0[r_x + i, r_y : r_y + 2, :] = rcn[k, 13 + 2 * i : 15 + 2 * i, :]

    ops0 = (cx0, cy0, cz0, rd0, d0)
    build(m0, cx0, cy0, cz0, rd0, d0, 1, xs0 - 1, BASE_TAU, nz, 1)

    def first0(a):
        us0[a] = rd0[a] * rs0[a]
        uc0[a] = rd0[a] * rc0[a]

    slabs(1, xs0 - 1, 1, first0)
    sweep((us0, uc0), (vs0, vc0), (rs0, rc0), ops0, 2, xs0 - 2, 1)

    def down0(i, carry):
        num, den = carry
        sums = []
        for k in range(2):
            a = H0 + 2 * i + k
            vs, es = residual(vs0, rs0, a, ops0)
            vc, ec = residual(vc0, rc0, a, ops0)
            rs = rs0[a]
            num = num + fold((ec * vs + vc * rs)[H0 : H0 + by])
            den = den + fold((es * vs + vs * rs)[H0 : H0 + by])
            sums.append((es, ec))
        at = pl.ds(pl.multiple_of(i * by, by), by)
        t0[0, at, :] = (sums[0][0] + sums[1][0])[H0 : H0 + by]
        t0[1, at, :] = (sums[0][1] + sums[1][1])[H0 : H0 + by]
        return num, den

    zero8 = jnp.zeros((8, 128), F32)
    num0, den0 = lax.fori_loop(0, b1x, down0, (zero8, zero8))
    for v in range(2):
        t0y[...] = mm(t0[v], zc0)
        coarse = 0.125 * pair_rows(t0y, b1x * b1y)
        for i in range(b1x):
            r1[v, H1 + i, b1y : 2 * b1y, :] = coarse[i * b1y : (i + 1) * b1y]
    each(lambda k: level1_copies(r1, e1s, e1r, k, False, 4), start)

    each(lambda k: level1_copies(m1, m1s, m1r, k, True, 5), lambda c: c.wait_recv())
    ops1 = (cx1, cy1, cz1, rd1, d1)
    build(m1.at[0], cx1, cy1, cz1, rd1, d1, 1, b1x + 2 * H1 - 1, BASE_TAU / 4, z1, 2)
    over_wide(*gather_m, "recv")
    over_narrow(*spread_m, "start")

    each(lambda k: level1_copies(r1, e1s, e1r, k, True, 4), lambda c: c.wait_recv())
    rr1 = (r1.at[0], r1.at[1])
    uu1 = (u1.at[0], u1.at[1])
    vv1 = (v1.at[0], v1.at[1])

    def first1(a):
        for v in range(2):
            u1[v, a] = rd1[a] * r1[v, a]

    slabs(1, b1x + 2 * H1 - 1, 2, first1)
    sweep(uu1, vv1, rr1, ops1, 2, b1x + 2 * H1 - 2, 2)
    num1, den1 = zero8, zero8
    own_y = slice(b1y, 2 * b1y)
    for i in range(b2x):
        pair = []
        for k in range(2):
            a = H1 + 2 * i + k
            vs, es = residual(vv1[0], rr1[0], a, ops1)
            vc, ec = residual(vv1[1], rr1[1], a, ops1)
            rs = r1[0, a]
            num1 = num1 + fold((ec * vs + vc * rs)[own_y])
            den1 = den1 + fold((es * vs + vs * rs)[own_y])
            pair.append((es, ec))
        for v in range(2):
            t1[v, i * b1y : (i + 1) * b1y, :] = (pair[0][v] + pair[1][v])[own_y]
    t1y[...] = mm(t1[0], zc1) + mm(t1[1], zc1b)
    own2 = 0.125 * pair_rows(t1y, b2x * b2y)
    sr2[...] = own2
    gr[ino, iw] = own2
    num_row = jnp.sum(num0 + 8.0 * num1, axis=0, keepdims=True)
    den_row = jnp.sum(den0 + 8.0 * den1, axis=0, keepdims=True)
    row8 = iota((8, 128), 0)
    part = jnp.where(row8 == 0, num_row, jnp.where(row8 == 1, den_row, 0.0))
    sp2[...] = part
    gp[iw] = part
    over_wide(*gather_r, "start")
    over_wide(*gather_p, "start")

    over_narrow(*spread_m, "recv")

    def unpack(src, dst):
        def step(w, _):
            for n in range(nn):
                for i in range(b2x):
                    dst[PAD + w * b2x + i, n * b2y : (n + 1) * b2y, :] = src[n, w, i * b2y : (i + 1) * b2y, :]
            return 0

        lax.fori_loop(0, nw, step, 0)

    unpack(gm, v2)
    build(v2, cx2, cy2, cz2, rd2, None, PAD, PAD + x2, BASE_TAU / 16, z2, 4)

    def coarsen_pairs(get, xc, rows, dst):
        half = rows // 2

        def step(g, _):
            for k in range(4):
                a = PAD + 2 * (4 * g + k)
                t2[k * rows : (k + 1) * rows, :] = get(a) + get(a + 1)
            t2y[0 : 4 * rows, :] = mm(t2[0 : 4 * rows, :], zc1)
            flat = 0.125 * (t2y[pl.ds(0, 4 * half, stride=2), :] + t2y[pl.ds(1, 4 * half, stride=2), :])
            for k in range(4):
                dst[PAD + 4 * g + k, 0:half, :] = flat[k * half : (k + 1) * half]
            return 0

        lax.fori_loop(0, xc // 4, step, 0)

    v4[...] = jnp.zeros(v4.shape, F32)
    r4[...] = jnp.zeros(r4.shape, F32)
    coarsen_pairs(lambda a: v2[a], x3, v2.shape[1], v3)
    build(v3, cx3, cy3, cz3, rd3, None, PAD, PAD + x3, BASE_TAU / 64, z2 // 2, 4)
    coarsen_pairs(lambda a: v3[a], x4, v3.shape[1], v4)
    build(v4, cx4, cy4, cz4, rd4, None, PAD, PAD + x4, BASE_TAU / 256, z2 // 4, 4)

    over_wide(*gather_r, "recv")
    over_narrow(*spread_r, "start")
    over_wide(*gather_p, "recv")
    total = gp[0]
    if nw <= 16:
        for w in range(1, nw):
            total = total + gp[w]
    else:
        total = lax.fori_loop(1, nw, lambda w, acc: acc + gp[w], total)
    pb[...] = total
    over_narrow(*spread_p, "start")
    over_narrow(*spread_r, "recv")
    unpack(gr, r2)

    ops2 = (cx2, cy2, cz2, rd2, None)
    ops3 = (cx3, cy3, cz3, rd3, None)
    ops4 = (cx4, cy4, cz4, rd4, None)

    def down(u, v, r, ops, xc):
        def first(a):
            u[a] = ops[3][a] * r[a]

        slabs(PAD, PAD + xc, 4, first)
        sweep((u,), (v,), (r,), ops, PAD, PAD + xc, 4)

    def up(v, coarse, xc, rows):
        half = rows // 2

        def step(g, _):
            for k in range(4):
                t2[8 * k : 8 * k + 8, :] = coarse[PAD + 4 * g + k]
            wide_rows = mm(t2[0:32, :], zr)
            t2y[pl.ds(0, 32, stride=2), :] = wide_rows
            t2y[pl.ds(1, 32, stride=2), :] = wide_rows
            for k in range(4):
                add = t2y[16 * k : 16 * k + rows, :]
                a = PAD + 2 * (4 * g + k)
                v[a] = v[a] + add
                v[a + 1] = v[a + 1] + add
            return 0

        lax.fori_loop(0, xc // 4, step, 0)

    down(u2, v2, r2, ops2, x2)
    coarsen_pairs(lambda a: residual(v2, r2, a, ops2)[1], x3, v2.shape[1], r3)
    down(u3, v3, r3, ops3, x3)
    coarsen_pairs(lambda a: residual(v3, r3, a, ops3)[1], x4, v3.shape[1], r4)
    down(u4, v4, r4, ops4, x4)
    up(v3, v4, x4, v3.shape[1])
    sweep((v3,), (u3,), (r3,), ops3, PAD, PAD + x3, 4)
    sweep((u3,), (v3,), (r3,), ops3, PAD, PAD + x3, 4)
    up(v2, v3, x3, v2.shape[1])
    sweep((v2,), (u2,), (r2,), ops2, PAD, PAD + x2, 4)
    sweep((u2,), (v2,), (r2,), ops2, PAD, PAD + x2, 4)

    low = iota(v2.shape[1:], 1) < z2

    def dots(i, carry):
        num, den = carry
        for k in range(4):
            a = PAD + 4 * i + k
            both = jnp.where(low, v2[a], 0.0)
            den = den + fold(both * r2[a])
            num = num + fold(both * shift(r2[a], z2, 1))
        return num, den

    num2, den2 = lax.fori_loop(0, x2 // 4, dots, (zero8, zero8))
    over_narrow(*spread_p, "recv")
    whole = total
    for j in range(1, nn):
        whole = whole + pbs[lax.rem(ino + j, nn)]
    num = jnp.sum(jnp.where(row8 == 0, whole, 0.0) + 64.0 * num2)
    den = jnp.sum(jnp.where(row8 == 1, whole, 0.0) + 64.0 * den2)
    ratio = (jnp.full((8, 128), num) / (1.0 + jnp.full((8, 128), den)))[0:1, :]

    rows2 = v2.shape[1]
    full_y = 2 * rows2
    for i in range(b2x + 4):
        e = v2[PAD + iw * b2x - 2 + i]
        f1[i * rows2 : (i + 1) * rows2, :] = shift(e, z2, 1) - ratio * e
    fine = mm(f1[...], zr)
    for i in range(b2x + 4):
        part = fine[i * rows2 : (i + 1) * rows2]
        f1p[i, 0:b1y, :] = jnp.zeros((b1y, z1), F32)
        f1p[i, b1y + full_y : 2 * b1y + full_y, :] = jnp.zeros((b1y, z1), F32)
        f1p[i, pl.ds(b1y, rows2, stride=2), :] = part
        f1p[i, pl.ds(b1y + 1, rows2, stride=2), :] = part
    window = pl.ds(pl.multiple_of(ino * b1y, 8), 3 * b1y)
    for a in range(2, b1x + 2 * H1 - 2):
        i = (a - H1) // 2 + 2
        u1[0, a] = v1[1, a] - ratio * v1[0, a] + f1p[i, window, :]
        w1[a] = r1[1, a] - ratio * r1[0, a]
    sweep((u1.at[0],), (u1.at[1],), (w1,), ops1, 3, b1x + 2 * H1 - 3, 2)
    sweep((u1.at[1],), (u1.at[0],), (w1,), ops1, 4, b1x + 2 * H1 - 4, 2)

    rows1 = 3 * b1y
    zr0 = spread_matrix(z1, nz)
    ratio0 = jnp.concatenate([ratio] * (nz // 128), axis=1)
    for i in range(b1x + 2):
        part = mm(u1[0, H1 - 1 + i], zr0)
        for ref, lanes in ((f0a, slice(0, 128)), (f0b, slice(128, 256))):
            ref[i, pl.ds(0, rows1, stride=2), :] = part[:, lanes]
            ref[i, pl.ds(1, rows1, stride=2), :] = part[:, lanes]
    y_at = 2 * b1y - H0

    def up0(i, _):
        add = jnp.concatenate([f0a[i, y_at : y_at + m0.shape[1], :], f0b[i, y_at : y_at + m0.shape[1], :]], axis=1)
        for k in range(2):
            a = H0 - 2 + 2 * i + k
            us0[a] = vc0[a] - ratio0 * vs0[a] + add
            rc0[a] = rc0[a] - ratio0 * rs0[a]
        return 0

    lax.fori_loop(0, b1x + 2, up0, 0)
    sweep((us0,), (uc0,), (rc0,), ops0, 3, xs0 - 3, 1)

    def last(a):
        own, t = neighbours(uc0, a, cx0, cy0, cz0)
        out_ref[a - H0] = (KEEP * own + rd0[a] * (rc0[a] + t))[H0 : H0 + by]

    slabs(H0, H0 + bx, 1, last)

    each(lambda k: e0_copies(k, False), lambda c: c.wait_send())
    each(lambda k: level1_copies(m1, m1s, m1r, k, False, 5), lambda c: c.wait_send())
    each(lambda k: level1_copies(r1, e1s, e1r, k, False, 4), lambda c: c.wait_send())
    over_wide(*gather_m, "send")
    over_wide(*gather_r, "send")
    over_wide(*gather_p, "send")
    over_narrow(*spread_m, "send")
    over_narrow(*spread_r, "send")
    over_narrow(*spread_p, "send")


def solution(mesh):
    nw, nn = mesh.shape["wide"], mesh.shape["narrow"]

    def per_device(mobility, sav_vector, cotangent):
        bx, by, nz = mobility.shape
        b1x, b1y, z1 = bx // 2, by // 2, nz // 2
        x2, y2 = nw * bx // 4, nn * by // 4
        vm = lambda *s: pltpu.VMEM(s, F32)
        dma = lambda *s: pltpu.SemaphoreType.DMA(s)
        l0 = (bx + 2 * H0, by + 2 * H0, nz)
        l1 = (b1x + 2 * H1, 3 * b1y, z1)
        l2 = (x2 + 2 * PAD, y2, z1)
        l3 = (x2 // 2 + 2 * PAD, y2 // 2, z1)
        l4 = (x2 // 4 + 2 * PAD, 8, z1)
        own2 = (bx // 4 * (by // 4), z1)
        scratch = (
            [vm(*l0)] * 12
            + [vm(2, 10, bx, nz), vm(2, 10, bx, nz), vm(2, 10, bx, nz), vm(4, 24, nz), vm(4, 24, nz)]
            + [vm(1, *l1)] + [vm(*l1)] * 5 + [vm(2, *l1)] * 3 + [vm(*l1)]
            + [vm(*l2)] * 7 + [vm(*l3)] * 7 + [vm(*l4)] * 7
            + [vm(2, b1x * by, nz), vm(b1x * by, z1), vm(2, bx // 4 * b1y, z1), vm(bx // 4 * b1y, z1)]
            + [vm(*own2), vm(*own2), vm(8, 128), vm(nn, nw, *own2), vm(nn, nw, *own2), vm(nw, 8, 128),
               vm(8, 128), vm(nn, 8, 128)]
            + [vm(64, z1), vm(64, z1)]
            + [vm((bx // 4 + 4) * y2, z1), vm(bx // 4 + 4, 2 * y2 + 2 * b1y, z1)]
            + [vm(b1x + 2, 6 * b1y, 128)] * 2
            + [dma(8, 3), dma(8, 3), dma(8, 1), dma(8, 1), dma(8, 2), dma(8, 2)]
            + [dma(nw), dma(nw), dma(nn), dma(nn)] + [dma(nw)] * 4 + [dma(nn)] * 4
        )
        return pl.pallas_call(
            functools.partial(kernel, nw, nn, bx, by, nz),
            out_shape=jax.ShapeDtypeStruct((bx, by, nz), F32),
            in_specs=[pl.BlockSpec(memory_space=pltpu.VMEM)] * 3,
            out_specs=pl.BlockSpec(memory_space=pltpu.VMEM),
            scratch_shapes=scratch,
            compiler_params=pltpu.CompilerParams(
                collective_id=0, has_side_effects=True, vmem_limit_bytes=67043328
            ),
        )(mobility, sav_vector, cotangent)

    spec = P("wide", "narrow", None)
    return jax.shard_map(per_device, mesh=mesh, in_specs=(spec,) * 3, out_specs=spec, check_vma=False)
```

time: 463 us -> 54.8 us (0.12)
  starting transfers between devices: 281 us -> 0 us
  local copies, waits for them, and re-layouts: 74.9 us -> 1.67 us
  Pallas kernels: 0 us -> 53 us
  blocking collectives: 45.1 us -> 0 us
  other arithmetic: 34.1 us -> 0 us
  waiting for transfers between devices: 20.2 us -> 0 us
    ppermute x88 -> x0, starting transfers between devices: 281 us -> none  [the longest x44 208 us: with_halo(): lax.ppermute(lax.slice_in_dim(block, block.shape[dim] - width, None, axis...]
    pallas_call x0 -> x1, Pallas kernels: none -> 53 us  [per_device(): pl.pallas_call(functools.partial(kernel, nw, nn, bx, by, nz), out_shape=j...]
    reshape x9 -> x0, local copies, waits for them, and re-layouts: 47.1 us -> none  [the longest x3 40.9 us: coarsen(): values.reshape(count, size_x // 2, 2, size_y // 2, 2, size_z // 2, 2)]
    psum x1 -> x0, blocking collectives: 45.1 us -> none  [inner_sums(): lax.psum((jnp.sum(adjoint_b * cotangent), jnp.sum(sav_vector * adjoint_b)...]
    reduce_sum x10 -> x0, other arithmetic: 23.2 us -> none  [the longest x9 22.5 us: coarsen(): return blocks.mean(axis=(2, 4, 6))]
    ppermute x88 -> x0, waiting for transfers between devices: 20.2 us -> none  [the longest x44 20.1 us: with_halo(): lax.ppermute(lax.slice_in_dim(block, block.shape[dim] - width, None, axis...]
    another operation x1 -> x0, local copies, waits for them, and re-layouts: 18.9 us -> none  [coarsen(): values.reshape(count, size_x // 2, 2, size_y // 2, 2, size_z // 2, 2)]
    concatenate x43 -> x0, other arithmetic: 5.81 us -> none  [with_halo(): block = jnp.concatenate([low, block, high], axis=dim)]
  transfers between devices with their start and end apart: 88 -> 0, of which waited for: 27 -> 0; matrix products, arithmetic and copies ran while one was open for 20% -> 0% of each run, Pallas kernels for 0% -> 0%
where the time goes in v1:
time: 54.8 us; the launch traced here: 54.7 us
  Pallas kernels  53 us (97%)
  local copies, waits for them, and re-layouts  1.67 us (3%)
    pallas_call x1, Pallas kernels, per_device(): pl.pallas_call(functools.partial(kernel, nw, nn, bx, by, nz), out_shape=j...  53 us
    unnamed x1, local copies, waits for them, and re-layouts  1.67 us

profile of v1, /device:TPU:1, one launch (start us, length us, event | category | flops | bytes accessed | tf_op | source)
XLA Modules:
  0.0 54.7 jit_solution(17890779222131561548)
XLA Ops:
  0.0 53.0 %shard_map.37 = f32[16,16,256]{2,1,0:T(8,128)} custom-call(f32[16,16,256]{2,1,0:T(8,128)} %m_ref.1, f32[16,16,256]{2,1,0:T(8,128)} %s_ref.1, f32[16,16,256]{2,1,0:T(8,128)} %c_ref.1), custom_call_target="tpu_custom_call" | custom-call | tf_op jit(solution)/shard_map/pallas_call | solution.py:627
  53.0 1.7 %copy.5 = f32[16,16,256]{2,1,0:T(8,128)} copy(f32[16,16,256]{2,1,0:T(8,128)} %shard_map.37) | data formatting | bytes 524288

commit v2 on v1

--- a/solution.py
+++ b/solution.py
@@ -183,7 +183,7 @@
         return pltpu.make_async_remote_copy(src_ref=src, dst_ref=dst, send_sem=ssem, recv_sem=rsem,
                                             device_id=dev, device_id_type=MESH)
 
-    def e0_copies(side, recv):
+    def e0_copies(side, recv, wave=0):
         other = OPPOSITE[side]
         land = side if recv else other
         dev = peer(side)
@@ -192,8 +192,15 @@
             at = 0
             for n, (ref, width) in enumerate(((m_ref, 4), (s_ref, 3), (c_ref, 3))):
                 lo = 0 if side == 0 else bx - width
-                out.append(remote(ref.at[lo : lo + width], rx.at[land, at : at + width],
-                                  e0s.at[side, n], e0r.at[land, n], dev))
+                skip = width - 1 if side == 0 else 0
+                first = 0 if side == 0 else 1
+                if wave == 1:
+                    out.append(remote(ref.at[lo + skip : lo + skip + 1], rx.at[land, at + skip : at + skip + 1],
+                                      e0s.at[side, 3 + n], e0r.at[land, 3 + n], dev))
+                else:
+                    out.append(remote(ref.at[lo + first : lo + first + width - 1],
+                                      rx.at[land, at + first : at + first + width - 1],
+                                      e0s.at[side, n], e0r.at[land, n], dev))
                 at += width
             return out
         if side < 4:
@@ -218,8 +225,8 @@
         return [remote(ref.at[v, sx : sx + w, sy : sy + b1y], ref.at[v, tx : tx + w, ty : ty + b1y],
                        ssem.at[side, v], rsem.at[land, v], peer(side)) for v in range(ref.shape[0])]
 
-    def each(fn, act):
-        for side in range(8):
+    def each(fn, act, sides=range(8)):
+        for side in sides:
             @pl.when(there[side])
             def _():
                 for copy in fn(side):
@@ -228,7 +235,7 @@
     def start(copy):
         copy.start()
 
-    each(lambda k: e0_copies(k, False), start)
+    each(lambda k: e0_copies(k, False), start, (0, 1, 4, 5, 6, 7, 2, 3))
 
     zc0 = squeeze_matrix(nz, z1)
     zc1 = squeeze_matrix(z1, z1)
@@ -299,6 +306,7 @@
     gather_p = (sp2, lambda w: gp.at[w], aps, apr)
     spread_r = (gr.at[ino], lambda n: gr.at[n], brs, brr)
     spread_p = (pb, lambda n: pbs.at[n], bps, bpr)
+    each(lambda k: e0_copies(k, False, 1), start, (0, 1))
     over_wide(*gather_m, "start")
 
     blank = jnp.zeros((H0, m0.shape[1], nz), F32)
@@ -330,32 +338,29 @@
         def _():
             rcn[k] = jnp.zeros(rcn.shape[1:], F32)
 
-    each(lambda k: e0_copies(k, True), lambda c: c.wait_recv())
-    for k, ref, at, width in ((0, m0, 0, 4), (0, rs0, 4, 3), (0, rc0, 7, 3)):
+    def landed(copy):
+        copy.wait_recv()
+
+    each(lambda k: e0_copies(k, True), landed, (2, 3))
+    fields = ((m0, 0, 4), (rs0, 4, 3), (rc0, 7, 3))
+    for ref, at, width in fields:
         for i in range(width):
-            ref[H0 - width + i, H0 : H0 + by, :] = rx[0, at + i]
-            ref[H0 + bx + i, H0 : H0 + by, :] = rx[1, at + i]
             ref[H0 : H0 + bx, H0 - width + i, :] = ry[0, at + i]
             ref[H0 : H0 + bx, H0 + by + i, :] = ry[1, at + i]
-    for k in range(4):
-        dx, dy = SIDES[4 + k]
-        m_x, m_y = (H0 - 3 if dx < 0 else H0 + bx), (H0 - 3 if dy < 0 else H0 + by)
-        r_x, r_y = (H0 - 2 if dx < 0 else H0 + bx), (H0 - 2 if dy < 0 else H0 + by)
-        for i in range(3):
-            m0[m_x + i, m_y : m_y + 3, :] = rcn[k, 3 * i : 3 * i + 3, :]
-        for i in range(2):
-            rs0[r_x + i, r_y : r_y + 2, :] = rcn[k, 9 + 2 * i : 11 + 2 * i, :]
-            rc0[r_x + i, r_y : r_y + 2, :] = rcn[k, 13 + 2 * i : 15 + 2 * i, :]
 
     ops0 = (cx0, cy0, cz0, rd0, d0)
-    build(m0, cx0, cy0, cz0, rd0, d0, 1, xs0 - 1, BASE_TAU, nz, 1)
 
     def first0(a):
         us0[a] = rd0[a] * rs0[a]
         uc0[a] = rd0[a] * rc0[a]
 
-    slabs(1, xs0 - 1, 1, first0)
-    sweep((us0, uc0), (vs0, vc0), (rs0, rc0), ops0, 2, xs0 - 2, 1)
+    def start0(lo, hi, v_lo, v_hi):
+        build(m0, cx0, cy0, cz0, rd0, d0, lo, hi, BASE_TAU, nz, 1)
+        slabs(lo, hi, 1, first0)
+        if v_hi > v_lo:
+            sweep((us0, uc0), (vs0, vc0), (rs0, rc0), ops0, v_lo, v_hi, 1)
+
+    start0(H0 + 1, H0 + bx - 1, H0 + 2, H0 + bx - 2)
 
     def down0(i, carry):
         num, den = carry
@@ -374,7 +379,28 @@
         return num, den
 
     zero8 = jnp.zeros((8, 128), F32)
-    num0, den0 = lax.fori_loop(0, b1x, down0, (zero8, zero8))
+    part0 = lax.fori_loop(2, b1x - 2, down0, (zero8, zero8))
+
+    each(lambda k: e0_copies(k, True), landed, (0, 1, 4, 5, 6, 7))
+    for ref, at, width in fields:
+        for i in range(width - 1):
+            ref[H0 - width + 1 + i, H0 : H0 + by, :] = rx[0, at + 1 + i]
+            ref[H0 + bx + i, H0 : H0 + by, :] = rx[1, at + i]
+    for k in range(4):
+        dx, dy = SIDES[4 + k]
+        m_x, m_y = (H0 - 3 if dx < 0 else H0 + bx), (H0 - 3 if dy < 0 else H0 + by)
+        r_x, r_y = (H0 - 2 if dx < 0 else H0 + bx), (H0 - 2 if dy < 0 else H0 + by)
+        for i in range(3):
+            m0[m_x + i, m_y : m_y + 3, :] = rcn[k, 3 * i : 3 * i + 3, :]
+        for i in range(2):
+            rs0[r_x + i, r_y : r_y + 2, :] = rcn[k, 9 + 2 * i : 11 + 2 * i, :]
+            rc0[r_x + i, r_y : r_y + 2, :] = rcn[k, 13 + 2 * i : 15 + 2 * i, :]
+    for lo, hi, v_lo, v_hi in ((2, H0 + 1, 3, H0 + 2), (H0 + bx - 1, xs0 - 2, H0 + bx - 2, xs0 - 3)):
+        build(m0, cx0, cy0, cz0, rd0, d0, lo, hi, BASE_TAU, nz, 1)
+        slabs(lo, hi, 1, first0)
+        sweep((us0, uc0), (vs0, vc0), (rs0, rc0), ops0, v_lo, v_hi, 1)
+    part0 = lax.fori_loop(0, 2, down0, part0)
+    num0, den0 = lax.fori_loop(b1x - 2, b1x, down0, part0)
     for v in range(2):
         t0y[...] = mm(t0[v], zc0)
         coarse = 0.125 * pair_rows(t0y, b1x * b1y)
@@ -382,6 +408,12 @@
             r1[v, H1 + i, b1y : 2 * b1y, :] = coarse[i * b1y : (i + 1) * b1y]
     each(lambda k: level1_copies(r1, e1s, e1r, k, False, 4), start)
 
+    each(lambda k: e0_copies(k, True, 1), landed, (0, 1))
+    for ref, at, width in fields:
+        ref[H0 - width, H0 : H0 + by, :] = rx[0, at]
+        ref[H0 + bx + width - 1, H0 : H0 + by, :] = rx[1, at + width - 1]
+    for lo, v_lo in ((1, 2), (xs0 - 2, xs0 - 3)):
+        start0(lo, lo + 1, v_lo, v_lo + 1)
     each(lambda k: level1_copies(m1, m1s, m1r, k, True, 5), lambda c: c.wait_recv())
     ops1 = (cx1, cy1, cz1, rd1, d1)
     build(m1.at[0], cx1, cy1, cz1, rd1, d1, 1, b1x + 2 * H1 - 1, BASE_TAU / 4, z1, 2)
@@ -585,6 +617,7 @@
     slabs(H0, H0 + bx, 1, last)
 
     each(lambda k: e0_copies(k, False), lambda c: c.wait_send())
+    each(lambda k: e0_copies(k, False, 1), lambda c: c.wait_send(), (0, 1))
     each(lambda k: level1_copies(m1, m1s, m1r, k, False, 5), lambda c: c.wait_send())
     each(lambda k: level1_copies(r1, e1s, e1r, k, False, 4), lambda c: c.wait_send())
     over_wide(*gather_m, "send")
@@ -621,7 +654,7 @@
             + [vm(64, z1), vm(64, z1)]
             + [vm((bx // 4 + 4) * y2, z1), vm(bx // 4 + 4, 2 * y2 + 2 * b1y, z1)]
             + [vm(b1x + 2, 6 * b1y, 128)] * 2
-            + [dma(8, 3), dma(8, 3), dma(8, 1), dma(8, 1), dma(8, 2), dma(8, 2)]
+            + [dma(8, 6), dma(8, 6), dma(8, 1), dma(8, 1), dma(8, 2), dma(8, 2)]
             + [dma(nw), dma(nw), dma(nn), dma(nn)] + [dma(nw)] * 4 + [dma(nn)] * 4
         )
         return pl.pallas_call(

time: 54.8 us -> 50.2 us (0.916)
  Pallas kernels: 53 us -> 48.4 us
    pallas_call x1, Pallas kernels: 53 us -> 48.4 us  [per_device(): pl.pallas_call(functools.partial(kernel, nw, nn, bx, by, nz), out_shape=j...]
where the time goes in v2:
time: 50.2 us; the launch traced here: 50.1 us
  Pallas kernels  48.4 us (96%)
  local copies, waits for them, and re-layouts  1.67 us (3%)
    pallas_call x1, Pallas kernels, per_device(): pl.pallas_call(functools.partial(kernel, nw, nn, bx, by, nz), out_shape=j...  48.4 us
    unnamed x1, local copies, waits for them, and re-layouts  1.67 us

profile of v2, /device:TPU:1, one launch (start us, length us, event | category | flops | bytes accessed | tf_op | source)
XLA Modules:
  0.0 50.1 jit_solution(1793957420314717673)
XLA Ops:
  0.0 48.4 %shard_map.37 = f32[16,16,256]{2,1,0:T(8,128)} custom-call(f32[16,16,256]{2,1,0:T(8,128)} %m_ref.1, f32[16,16,256]{2,1,0:T(8,128)} %s_ref.1, f32[16,16,256]{2,1,0:T(8,128)} %c_ref.1), custom_call_target="tpu_custom_call" | custom-call | tf_op jit(solution)/shard_map/pallas_call | solution.py:660
  48.4 1.7 %copy.5 = f32[16,16,256]{2,1,0:T(8,128)} copy(f32[16,16,256]{2,1,0:T(8,128)} %shard_map.37) | data formatting | bytes 524288

commit v3 on v2

--- a/solution.py
+++ b/solution.py
@@ -81,6 +81,10 @@
             d[a] = total
 
     slabs(lo, hi, chunk, body)
+
+
+def pairs(lo, hi):
+    return 2 - (hi - lo) % 2
 
 
 def neighbours(v, a, cx, cy, cz):
@@ -355,10 +359,10 @@
         uc0[a] = rd0[a] * rc0[a]
 
     def start0(lo, hi, v_lo, v_hi):
-        build(m0, cx0, cy0, cz0, rd0, d0, lo, hi, BASE_TAU, nz, 1)
+        build(m0, cx0, cy0, cz0, rd0, d0, lo, hi, BASE_TAU, nz, pairs(lo, hi))
         slabs(lo, hi, 1, first0)
         if v_hi > v_lo:
-            sweep((us0, uc0), (vs0, vc0), (rs0, rc0), ops0, v_lo, v_hi, 1)
+            sweep((us0, uc0), (vs0, vc0), (rs0, rc0), ops0, v_lo, v_hi, pairs(v_lo, v_hi))
 
     start0(H0 + 1, H0 + bx - 1, H0 + 2, H0 + bx - 2)
 
@@ -396,9 +400,9 @@
             rs0[r_x + i, r_y : r_y + 2, :] = rcn[k, 9 + 2 * i : 11 + 2 * i, :]
             rc0[r_x + i, r_y : r_y + 2, :] = rcn[k, 13 + 2 * i : 15 + 2 * i, :]
     for lo, hi, v_lo, v_hi in ((2, H0 + 1, 3, H0 + 2), (H0 + bx - 1, xs0 - 2, H0 + bx - 2, xs0 - 3)):
-        build(m0, cx0, cy0, cz0, rd0, d0, lo, hi, BASE_TAU, nz, 1)
+        build(m0, cx0, cy0, cz0, rd0, d0, lo, hi, BASE_TAU, nz, pairs(lo, hi))
         slabs(lo, hi, 1, first0)
-        sweep((us0, uc0), (vs0, vc0), (rs0, rc0), ops0, v_lo, v_hi, 1)
+        sweep((us0, uc0), (vs0, vc0), (rs0, rc0), ops0, v_lo, v_hi, pairs(v_lo, v_hi))
     part0 = lax.fori_loop(0, 2, down0, part0)
     num0, den0 = lax.fori_loop(b1x - 2, b1x, down0, part0)
     for v in range(2):
@@ -470,7 +474,7 @@
         lax.fori_loop(0, nw, step, 0)
 
     unpack(gm, v2)
-    build(v2, cx2, cy2, cz2, rd2, None, PAD, PAD + x2, BASE_TAU / 16, z2, 4)
+    build(v2, cx2, cy2, cz2, rd2, None, PAD, PAD + x2, BASE_TAU / 16, z2, 8)
 
     def coarsen_pairs(get, xc, rows, dst):
         half = rows // 2
@@ -517,7 +521,7 @@
             u[a] = ops[3][a] * r[a]
 
         slabs(PAD, PAD + xc, 4, first)
-        sweep((u,), (v,), (r,), ops, PAD, PAD + xc, 4)
+        sweep((u,), (v,), (r,), ops, PAD, PAD + xc, 8)
 
     def up(v, coarse, xc, rows):
         half = rows // 2
@@ -543,11 +547,11 @@
     coarsen_pairs(lambda a: residual(v3, r3, a, ops3)[1], x4, v3.shape[1], r4)
     down(u4, v4, r4, ops4, x4)
     up(v3, v4, x4, v3.shape[1])
-    sweep((v3,), (u3,), (r3,), ops3, PAD, PAD + x3, 4)
-    sweep((u3,), (v3,), (r3,), ops3, PAD, PAD + x3, 4)
+    sweep((v3,), (u3,), (r3,), ops3, PAD, PAD + x3, 8)
+    sweep((u3,), (v3,), (r3,), ops3, PAD, PAD + x3, 8)
     up(v2, v3, x3, v2.shape[1])
-    sweep((v2,), (u2,), (r2,), ops2, PAD, PAD + x2, 4)
-    sweep((u2,), (v2,), (r2,), ops2, PAD, PAD + x2, 4)
+    sweep((v2,), (u2,), (r2,), ops2, PAD, PAD + x2, 8)
+    sweep((u2,), (v2,), (r2,), ops2, PAD, PAD + x2, 8)
 
     low = iota(v2.shape[1:], 1) < z2
 
@@ -608,13 +612,13 @@
         return 0
 
     lax.fori_loop(0, b1x + 2, up0, 0)
-    sweep((us0,), (uc0,), (rc0,), ops0, 3, xs0 - 3, 1)
+    sweep((us0,), (uc0,), (rc0,), ops0, 3, xs0 - 3, 2)
 
     def last(a):
         own, t = neighbours(uc0, a, cx0, cy0, cz0)
         out_ref[a - H0] = (KEEP * own + rd0[a] * (rc0[a] + t))[H0 : H0 + by]
 
-    slabs(H0, H0 + bx, 1, last)
+    slabs(H0, H0 + bx, 2, last)
 
     each(lambda k: e0_copies(k, False), lambda c: c.wait_send())
     each(lambda k: e0_copies(k, False, 1), lambda c: c.wait_send(), (0, 1))

time: 50.2 us -> 47.5 us (0.946)
  Pallas kernels: 48.4 us -> 45.7 us
    pallas_call x1, Pallas kernels: 48.4 us -> 45.7 us  [per_device(): pl.pallas_call(functools.partial(kernel, nw, nn, bx, by, nz), out_shape=j...]
where the time goes in v3:
time: 47.5 us; the launch traced here: 47.4 us
  Pallas kernels  45.7 us (96%)
  local copies, waits for them, and re-layouts  1.67 us (4%)
    pallas_call x1, Pallas kernels, per_device(): pl.pallas_call(functools.partial(kernel, nw, nn, bx, by, nz), out_shape=j...  45.7 us
    unnamed x1, local copies, waits for them, and re-layouts  1.67 us

profile of v3, /device:TPU:1, one launch (start us, length us, event | category | flops | bytes accessed | tf_op | source)
XLA Modules:
  0.0 47.4 jit_solution(1040264018355425948)
XLA Ops:
  0.0 45.7 %shard_map.37 = f32[16,16,256]{2,1,0:T(8,128)} custom-call(f32[16,16,256]{2,1,0:T(8,128)} %m_ref.1, f32[16,16,256]{2,1,0:T(8,128)} %s_ref.1, f32[16,16,256]{2,1,0:T(8,128)} %c_ref.1), custom_call_target="tpu_custom_call" | custom-call | tf_op jit(solution)/shard_map/pallas_call | solution.py:664
  45.7 1.7 %copy.5 = f32[16,16,256]{2,1,0:T(8,128)} copy(f32[16,16,256]{2,1,0:T(8,128)} %shard_map.37) | data formatting | bytes 524288
